TPU v7x, 32 devices: a whole 2x2x4 slice. The times are simulated.
32 devices in a mesh: scene: 2 (over x), mrow: 8 (over z, y), mcol: 2 (over core).
Axes of the slice: x: 2, y: 2, z: 4, core: 2. Of those that a mesh axis runs over, the one named last changes fastest.
Arguments:
- pan_blocks: bfloat16 [2048, 128, 128], P(('scene', 'mrow', 'mcol')), parts along dimension 0, may hold values from -6 to 6
- ms_blocks: bfloat16 [2048, 32, 256], P(('scene', 'mrow', 'mcol')), parts along dimension 0, may hold values from -6 to 6
- send_list: int32 [3, 2048], P(None, ('scene', 'mrow', 'mcol')), parts along dimension 1, may hold values from 0 to 127, as said below
- tile_list: int32 [3, 4096], P(None, ('scene', 'mrow', 'mcol')), parts along dimension 1, may hold values from 0 to 9, as said below
- row_grid: float32 [48], P(('scene', 'mrow')), parts along dimension 0, may hold values from -32 to 288
- col_grid: float32 [16, 16], P(('scene', 'mrow'), 'mcol'), parts along dimension 0, may hold values from -32 to 1312
- band_mix: float32 [8, 8], replicated, may hold values from -1.5 to 1.5
- band_gain: float32 [8], replicated, may hold values from 0.4 to 1.2
- synth_weight: float32 [8], replicated, may hold values from 0.05 to 0.3
Outputs:
- sharpened: bfloat16 [8, 2048, 1024], P(None, ('scene', 'mrow'), 'mcol'), parts along dimension 1
There are 2 independent parts, one for each index of `scene`. A program takes and returns all parts, laid end to end along the dimension named above; an argument that names none is the same for every part. Nothing has to cross between parts.
Inputs may be any that keep to these rules, and one draw needn't show every extreme that they name: `send_list`: row 0 gives each source block of a device a distinct send slot; slot p goes to map-row owner p // 16 in the device's own map column, so one device sends at most 16 blocks to one tile; in every draw one tile of each map column receives 16 blocks from every device of that column, and every device fills 16 slots of it. Row 1 is a cell row below 2; row 2 a cell column between mcol * 5 and mcol * 5 + 4. `tile_list`: row 0 is 1 exactly in the receive slots that send_list fills and 0 elsewhere; rows 1 and 2 repeat the cell row and column of the block sent there, and are 0 in empty slots.
All inputs are finite; a program needn't handle non-finite values.
Results may differ from a plain program's by a relative error of at most 0.0073.
Values may be sent and summed in bfloat16 or wider, within the bound.
A program may use at most 128 MiB of HBM per device.

v0:
```python
import jax
import jax.numpy as jnp
from jax import lax
from jax.sharding import PartitionSpec as P

GRID = 64
TR = 128
TC = 512


highest = lax.Precision.HIGHEST


def padded(cells, sides, width):
    for axis, dim in sides:
        count = lax.axis_size(axis)
        ends = count - 1
        head = lax.slice_in_dim(cells, 0, width, axis=dim)
        tail = lax.slice_in_dim(cells, cells.shape[dim] - width, cells.shape[dim], axis=dim)
        cells = jnp.concatenate(
            [
                lax.ppermute(tail, axis, [(i, (i + 1) % count) for i in range(ends)]),
                cells,
                lax.ppermute(head, axis, [((i + 1) % count, i) for i in range(ends)]),
            ],
            axis=dim,
        )
    return cells


def cubic_weight(offset):
    distance = jnp.abs(offset)
    near_part = (1.5 * distance - 2.5) * distance * distance + 1.0
    far_part = ((-0.5 * distance + 2.5) * distance - 4.0) * distance + 2.0
    return jnp.where(
        distance <= 1.0, near_part, jnp.where(distance < 2.0, far_part, jnp.zeros_like(distance))
    )


def along_nodes(node_values, position, offset, spacing):
    segment = jnp.minimum(position // spacing, node_values.shape[-1] - 2)
    left_node = jnp.take(node_values, segment, axis=-1)
    right_node = jnp.take(node_values, segment + 1, axis=-1)
    within = ((position - segment * spacing).astype(jnp.float32) + offset) / spacing
    return left_node + (right_node - left_node) * within


def source_weights(coords, cell_ids, block_size):
    pixels = (
        cell_ids[:, None, None] * block_size
        + jnp.arange(block_size, dtype=jnp.int32)[None, None, :]
    ).astype(jnp.float32)
    return cubic_weight(coords[:, :, None] - pixels).astype(jnp.bfloat16)


def row_weights(coords, cell_ids, is_valid, block_size):
    pixels = (
        cell_ids[None, :, None] * block_size
        + jnp.arange(block_size, dtype=jnp.int32)[None, None, :]
    ).astype(jnp.float32)
    return (cubic_weight(coords[:, None, None] - pixels) * is_valid[None, :, None]).astype(
        jnp.bfloat16
    )


def upsample_table(length, coarse):
    position = (jnp.arange(length, dtype=jnp.int32).astype(jnp.float32) - 1.5) * 0.25 + 2.0
    taps = jnp.arange(coarse + 4, dtype=jnp.int32).astype(jnp.float32)
    return cubic_weight(position[:, None] - taps[None, :]).astype(jnp.bfloat16)


def combine(upsampled, pan_map, band_mix, band_gain, synth_weight):
    mixture = jnp.transpose(upsampled, (1, 0, 2)) + jnp.einsum(
        "bk,rkc->brc", band_mix, upsampled, precision=highest
    )
    synthetic = jnp.einsum("k,rkc->rc", synth_weight, upsampled, precision=highest)
    return (mixture + band_gain[:, None, None] * (pan_map - synthetic)[None, :, :]).astype(
        jnp.bfloat16
    )


def column_pass(members):
    pan_data, ms_data, x_pan, x_ms, cell_ids = members
    block_size = pan_data.shape[1]
    coarse_size = ms_data.shape[1]
    band_count = ms_data.shape[2] // coarse_size
    col_weight = source_weights(x_pan, cell_ids, block_size)
    pan_cols = jnp.einsum(
        "sij,scj->sic", pan_data, col_weight, preferred_element_type=jnp.float32
    ).astype(jnp.bfloat16)
    spread = ms_data.reshape(ms_data.shape[0], coarse_size, band_count, coarse_size)
    ms_col_weight = source_weights(x_ms, cell_ids, coarse_size)
    ms_cols = jnp.einsum(
        "sibj,scj->sibc", spread, ms_col_weight, preferred_element_type=jnp.float32
    ).astype(jnp.bfloat16)
    return (pan_cols, ms_cols)


def grouped_pass(pan_data, ms_data, x_pan, x_ms, cell_ids):
    partition_total = pan_data.shape[0]
    groups = partition_total // 8
    stacked = (
        pan_data.reshape((groups, 8) + pan_data.shape[1:]),
        ms_data.reshape((groups, 8) + ms_data.shape[1:]),
        x_pan.reshape(groups, 8, x_pan.shape[1]),
        x_ms.reshape(groups, 8, x_ms.shape[1]),
        cell_ids.reshape(groups, 8),
    )
    pan_cols, ms_cols = lax.map(column_pass, stacked)
    return (
        pan_cols.reshape((partition_total,) + pan_cols.shape[2:]),
        ms_cols.reshape((partition_total,) + ms_cols.shape[2:]),
    )


def local(
    pan_blocks,
    ms_blocks,
    send_list,
    tile_list,
    row_grid,
    col_grid,
    band_mix,
    band_gain,
    synth_weight,
):
    row_owners = lax.axis_size("mrow")
    horizontal_location = lax.axis_index("mcol")
    own_blocks = pan_blocks.shape[0]
    partition_total = tile_list.shape[1]
    capacity = partition_total // row_owners
    block_size = pan_blocks.shape[1]
    coarse_size = ms_blocks.shape[1]
    band_count = band_gain.shape[0]
    coarse_rows = TR // 4
    coarse_cols = TC // 4
    band_nodes = lax.all_gather(col_grid, "mcol", axis=1, tiled=True)
    map_rows = jnp.arange(TR, dtype=jnp.int32)
    map_cols = horizontal_location * TC + jnp.arange(TC, dtype=jnp.int32)
    coarse_pos = horizontal_location * TC + 4 * jnp.arange(coarse_cols, dtype=jnp.int32) + 1
    y_pan = along_nodes(row_grid, map_rows, 0.0, GRID)
    y_ms = (
        along_nodes(row_grid, 4 * jnp.arange(coarse_rows, dtype=jnp.int32) + 1, 0.5, GRID) - 1.5
    ) * 0.25
    partition_number = send_list[0]
    owner_ids = (
        jnp.zeros((partition_total,), jnp.int32)
        .at[partition_number]
        .set(jnp.arange(own_blocks, dtype=jnp.int32))
    )
    filled = jnp.zeros((partition_total,), jnp.int32).at[partition_number].set(1) > 0
    zero_bf = jnp.zeros((), jnp.bfloat16)
    pan_send = jnp.where(filled[:, None, None], jnp.take(pan_blocks, owner_ids, axis=0), zero_bf)
    ms_send = jnp.where(filled[:, None, None], jnp.take(ms_blocks, owner_ids, axis=0), zero_bf)
    pan_recv, ms_recv = (
        lax.all_to_all(
            pan_send.reshape(row_owners, capacity, block_size, block_size),
            "mrow",
            split_axis=0,
            concat_axis=0,
            tiled=True,
        ),
        lax.all_to_all(
            ms_send.reshape(row_owners, capacity, coarse_size, ms_blocks.shape[2]),
            "mrow",
            split_axis=0,
            concat_axis=0,
            tiled=True,
        ),
    )
    x_pan = along_nodes(band_nodes[0], map_cols, 0.0, GRID)
    x_ms = (along_nodes(band_nodes[0], coarse_pos, 0.5, GRID) - 1.5) * 0.25
    pan_cols, ms_cols = grouped_pass(
        pan_recv.reshape(partition_total, block_size, block_size),
        ms_recv.reshape(partition_total, coarse_size, ms_blocks.shape[2]),
        jnp.broadcast_to(x_pan[None, :], (partition_total, TC)),
        jnp.broadcast_to(x_ms[None, :], (partition_total, coarse_cols)),
        tile_list[2],
    )
    is_valid = tile_list[0].astype(jnp.float32)
    cell_rows = tile_list[1]
    row_weight = row_weights(y_pan, cell_rows, is_valid, block_size)
    pan_map = jnp.dot(
        row_weight.reshape(TR, partition_total * block_size),
        pan_cols.reshape(partition_total * block_size, TC),
        preferred_element_type=jnp.float32,
    )
    ms_row_weight = row_weights(y_ms, cell_rows, is_valid, coarse_size)
    ms_map = jnp.dot(
        ms_row_weight.reshape(coarse_rows, partition_total * coarse_size),
        ms_cols.reshape(partition_total * coarse_size, band_count * coarse_cols),
        preferred_element_type=jnp.float32,
    ).astype(jnp.bfloat16)
    ms_map = ms_map.reshape(coarse_rows, band_count, coarse_cols)
    window = padded(ms_map, (("mrow", 0), ("mcol", 2)), 2)
    up_rows = upsample_table(TR, coarse_rows)
    up_cols = upsample_table(TC, coarse_cols)
    across = jnp.einsum("mbn,cn->mbc", window, up_cols, preferred_element_type=jnp.float32).astype(
        jnp.bfloat16
    )
    upsampled = jnp.dot(
        up_rows,
        across.reshape(coarse_rows + 4, band_count * TC),
        preferred_element_type=jnp.float32,
    ).reshape(TR, band_count, TC)
    return combine(upsampled, pan_map, band_mix, band_gain, synth_weight)


def solution(mesh):
    return jax.shard_map(
        local,
        mesh=mesh,
        in_specs=(
            P(("scene", "mrow", "mcol"), None, None),
            P(("scene", "mrow", "mcol"), None, None),
            P(None, ("scene", "mrow", "mcol")),
            P(None, ("scene", "mrow", "mcol")),
            P(("scene", "mrow")),
            P(("scene", "mrow"), "mcol"),
            P(),
            P(),
            P(),
        ),
        out_specs=P(None, ("scene", "mrow"), "mcol"),
        check_vma=False,
    )
```

profile of v0, /device:TPU:15, one launch (start us, length us, event | category | flops | bytes accessed | tf_op | source)
XLA Modules:
  0.0 289.1 jit_solution(7386547417058513332)
XLA Ops:
  2.6 3.2 %gather_fusion.1 = bf16[128,32,256]{2,1,0:T(8,128)(2,1)} fusion(bf16[64,32,256]{2,1,0:T(8,128)(2,1)} %param.20, s32[1024]{0:T(1024)S(1)} %pad_clamp_fusion), kind=kCustom, calls=%fused_computation.1 | custom fusion | bytes 4194816 | tf_op jit(solution)/shard_map/jit(_take)/gather | solution.py:154
  8.7 5.7 %all-to-all-start.1 = ((bf16[8,16,32,256]{3,2,1,0:T(8,128)(2,1)}), bf16[8,16,32,256]{3,2,1,0:T(8,128)(2,1)}, u32[]{:S(2)}, u32[]{:S(2)}) async-start(bf16[8,16,32,256]{3,2,1,0:T(8,128)(2,1)} %select_select_fusion.1), calls=%async_computation.1 | async-start | bytes 4194304 | tf_op jit(solution)/shard_map/all_to_all | solution.py:163
  14.3 3.0 %gather_fusion = bf16[128,128,128]{2,1,0:T(8,128)(2,1)} fusion(bf16[64,128,128]{2,1,0:T(8,128)(2,1)S(1)} %copy-done, s32[1024]{0:T(1024)S(1)} %pad_clamp_fusion), kind=kCustom, calls=%fused_computation | custom fusion | bytes 8389120 | tf_op jit(solution)/shard_map/jit(_take)/gather | solution.py:153
  17.4 3.9 %select_select_fusion = bf16[8,16,128,128]{3,2,1,0:T(8,128)(2,1)} fusion(bf16[8,16,128,128]{3,2,1,0:T(8,128)(2,1)} %bitcast.200, pred[8,16]{1,0:T(8,128)(4,1)S(1)} %broadcast_in_dim.148, pred[8,16]{1,0:T(8,128)(4,1)S(1)} %broadcast_in_dim.146), kind=kLoop, calls=%fused_computation.95 | loop fusion | flops 4194304 | bytes 8388864 | tf_op jit(solution)/shard_map/jit(_where)/select_n | solution.py:153
  21.2 38.8 %all-to-all-done.1 = bf16[8,16,32,256]{3,2,1,0:T(8,128)(2,1)} async-done(((bf16[8,16,32,256]{3,2,1,0:T(8,128)(2,1)}), bf16[8,16,32,256]{3,2,1,0:T(8,128)(2,1)}, u32[]{:S(2)}, u32[]{:S(2)}) %all-to-all-start.1) | async-done | bytes 2097184 | tf_op jit(solution)/shard_map/all_to_all | solution.py:163
  60.0 6.5 %all-to-all-start = ((bf16[8,16,128,128]{3,2,1,0:T(8,128)(2,1)}), bf16[8,16,128,128]{3,2,1,0:T(8,128)(2,1)}, u32[]{:S(2)}, u32[]{:S(2)}) async-start(bf16[8,16,128,128]{3,2,1,0:T(8,128)(2,1)} %select_select_fusion), calls=%async_computation | async-start | bytes 8388608 | tf_op jit(solution)/shard_map/all_to_all | solution.py:156
  68.4 4.0 %all-reduce = f32[16]{0:T(128)S(1)} all-reduce(f32[16]{0:T(128)S(1)} %bitcast_dynamic-update-slice_fusion), channel_id=1, replica_groups=mesh['scene'=2,'mrow'=8,'mcol'=2] {'mcol'}, use_global_device_ids=true, to_apply=%add | all-reduce | flops 16 | bytes 128 | tf_op jit(solution)/shard_map/squeeze | solution.py:171
  75.6 10.1 %add_multiply_fusion = f32[128]{0:T(128)S(1)} fusion(f32[]{:T(128)} %bitcast.39, f32[]{:T(128)} %bitcast.38, f32[]{:T(128)} %bitcast.37, f32[]{:T(128)} %bitcast.36, f32[]{:T(128)} %bitcast.35, f32[]{:T(128)} %bitcast.34, f32[]{:T(128)} %bitcast.33, f32[]{:T(128)} %bitcast.32, f32[]{:T(128)} %bitcast.31, f32[]{:T(128)} %bitcast.30, f32[]{:T(128)} %bitcast.29, ...), kind=kLoop, calls=%fused_computation.281 | loop fusion | flops 13312 | bytes 580 | tf_op jit(solution)/shard_map/mul | solution.py:172
  85.8 10.1 %fusion.154 = f32[512]{0:T(512)S(1)} fusion(f32[]{:T(128)} %bitcast.39, f32[]{:T(128)} %bitcast.38, f32[]{:T(128)} %bitcast.37, f32[]{:T(128)} %bitcast.36, f32[]{:T(128)} %bitcast.35, f32[]{:T(128)} %bitcast.34, f32[]{:T(128)} %bitcast.33, f32[]{:T(128)} %bitcast.32, f32[]{:T(128)} %bitcast.31, f32[]{:T(128)} %bitcast.30, f32[]{:T(128)} %bitcast.29, ...), kind=kLoop, calls=%fused_computation.201 | loop fusion | flops 50688 | bytes 2116 | tf_op jit(solution)/shard_map/add | solution.py:45
  96.3 60.9 %all-to-all-done = bf16[8,16,128,128]{3,2,1,0:T(8,128)(2,1)} async-done(((bf16[8,16,128,128]{3,2,1,0:T(8,128)(2,1)}), bf16[8,16,128,128]{3,2,1,0:T(8,128)(2,1)}, u32[]{:S(2)}, u32[]{:S(2)}) %all-to-all-start) | async-done | bytes 4194336 | tf_op jit(solution)/shard_map/all_to_all | solution.py:156
  157.2 95.9 %while.15 = (s32[]{:T(128)}, bf16[16,8,128,512]{3,2,1,0:T(8,128)(2,1)}, bf16[16,8,32,8,128]{4,3,2,1,0:T(8,128)(2,1)}, bf16[16,8,128,128]{3,2,1,0:T(8,128)(2,1)},...) while((s32[]{:T(128)}, ...), condition=%wide.region_3.7_spmd, body=%wide.region_2.6_spmd.sunk | while | flops 161810960 | bytes 2563853 | solution.py:109
  159.7 3.5 %fusion.223 = bf16[16,8,128,512]{3,2,1,0:T(8,128)(2,1)} fusion(bf16[16,8,128,512]{3,2,1,0:T(8,128)(2,1)} %get-tuple-element.249, s32[]{:T(128)} %get-tuple-element.248, f32[8,128]{1,0:T(8,128)S(1)} %add_convert_fusion.5, f32[8,512]{1,0:T(8,128)S(1)} %dynamic-slice_bitcast_fusion.4, bf16[16,8,128,128]{3,2,1,0:T(8,128)(2,1)} %get-tuple-element.260), kind=kOutput, calls=%fused_computation.13.clone.1 | convolution fusion | flops 144179200 | bytes 1332224 | tf_op jit(solution)/shard_map/while/body/eval_jaxpr/sij,scj->sic/dot_general | solution.py:88
  165.7 3.5 %fusion.223 = bf16[16,8,128,512]{3,2,1,0:T(8,128)(2,1)} fusion(bf16[16,8,128,512]{3,2,1,0:T(8,128)(2,1)} %get-tuple-element.249, s32[]{:T(128)} %get-tuple-element.248, f32[8,128]{1,0:T(8,128)S(1)} %add_convert_fusion.5, f32[8,512]{1,0:T(8,128)S(1)} %dynamic-slice_bitcast_fusion.4, bf16[16,8,128,128]{3,2,1,0:T(8,128)(2,1)} %get-tuple-element.260), kind=kOutput, calls=%fused_computation.13.clone.1 | convolution fusion | flops 144179200 | bytes 1332224 | tf_op jit(solution)/shard_map/while/body/eval_jaxpr/sij,scj->sic/dot_general | solution.py:88
  171.7 3.5 %fusion.223 = bf16[16,8,128,512]{3,2,1,0:T(8,128)(2,1)} fusion(bf16[16,8,128,512]{3,2,1,0:T(8,128)(2,1)} %get-tuple-element.249, s32[]{:T(128)} %get-tuple-element.248, f32[8,128]{1,0:T(8,128)S(1)} %add_convert_fusion.5, f32[8,512]{1,0:T(8,128)S(1)} %dynamic-slice_bitcast_fusion.4, bf16[16,8,128,128]{3,2,1,0:T(8,128)(2,1)} %get-tuple-element.260), kind=kOutput, calls=%fused_computation.13.clone.1 | convolution fusion | flops 144179200 | bytes 1332224 | tf_op jit(solution)/shard_map/while/body/eval_jaxpr/sij,scj->sic/dot_general | solution.py:88
  177.7 3.5 %fusion.223 = bf16[16,8,128,512]{3,2,1,0:T(8,128)(2,1)} fusion(bf16[16,8,128,512]{3,2,1,0:T(8,128)(2,1)} %get-tuple-element.249, s32[]{:T(128)} %get-tuple-element.248, f32[8,128]{1,0:T(8,128)S(1)} %add_convert_fusion.5, f32[8,512]{1,0:T(8,128)S(1)} %dynamic-slice_bitcast_fusion.4, bf16[16,8,128,128]{3,2,1,0:T(8,128)(2,1)} %get-tuple-element.260), kind=kOutput, calls=%fused_computation.13.clone.1 | convolution fusion | flops 144179200 | bytes 1332224 | tf_op jit(solution)/shard_map/while/body/eval_jaxpr/sij,scj->sic/dot_general | solution.py:88
  183.7 3.5 %fusion.223 = bf16[16,8,128,512]{3,2,1,0:T(8,128)(2,1)} fusion(bf16[16,8,128,512]{3,2,1,0:T(8,128)(2,1)} %get-tuple-element.249, s32[]{:T(128)} %get-tuple-element.248, f32[8,128]{1,0:T(8,128)S(1)} %add_convert_fusion.5, f32[8,512]{1,0:T(8,128)S(1)} %dynamic-slice_bitcast_fusion.4, bf16[16,8,128,128]{3,2,1,0:T(8,128)(2,1)} %get-tuple-element.260), kind=kOutput, calls=%fused_computation.13.clone.1 | convolution fusion | flops 144179200 | bytes 1332224 | tf_op jit(solution)/shard_map/while/body/eval_jaxpr/sij,scj->sic/dot_general | solution.py:88
  189.6 3.5 %fusion.223 = bf16[16,8,128,512]{3,2,1,0:T(8,128)(2,1)} fusion(bf16[16,8,128,512]{3,2,1,0:T(8,128)(2,1)} %get-tuple-element.249, s32[]{:T(128)} %get-tuple-element.248, f32[8,128]{1,0:T(8,128)S(1)} %add_convert_fusion.5, f32[8,512]{1,0:T(8,128)S(1)} %dynamic-slice_bitcast_fusion.4, bf16[16,8,128,128]{3,2,1,0:T(8,128)(2,1)} %get-tuple-element.260), kind=kOutput, calls=%fused_computation.13.clone.1 | convolution fusion | flops 144179200 | bytes 1332224 | tf_op jit(solution)/shard_map/while/body/eval_jaxpr/sij,scj->sic/dot_general | solution.py:88
  195.6 3.5 %fusion.223 = bf16[16,8,128,512]{3,2,1,0:T(8,128)(2,1)} fusion(bf16[16,8,128,512]{3,2,1,0:T(8,128)(2,1)} %get-tuple-element.249, s32[]{:T(128)} %get-tuple-element.248, f32[8,128]{1,0:T(8,128)S(1)} %add_convert_fusion.5, f32[8,512]{1,0:T(8,128)S(1)} %dynamic-slice_bitcast_fusion.4, bf16[16,8,128,128]{3,2,1,0:T(8,128)(2,1)} %get-tuple-element.260), kind=kOutput, calls=%fused_computation.13.clone.1 | convolution fusion | flops 144179200 | bytes 1332224 | tf_op jit(solution)/shard_map/while/body/eval_jaxpr/sij,scj->sic/dot_general | solution.py:88
  201.6 3.5 %fusion.223 = bf16[16,8,128,512]{3,2,1,0:T(8,128)(2,1)} fusion(bf16[16,8,128,512]{3,2,1,0:T(8,128)(2,1)} %get-tuple-element.249, s32[]{:T(128)} %get-tuple-element.248, f32[8,128]{1,0:T(8,128)S(1)} %add_convert_fusion.5, f32[8,512]{1,0:T(8,128)S(1)} %dynamic-slice_bitcast_fusion.4, bf16[16,8,128,128]{3,2,1,0:T(8,128)(2,1)} %get-tuple-element.260), kind=kOutput, calls=%fused_computation.13.clone.1 | convolution fusion | flops 144179200 | bytes 1332224 | tf_op jit(solution)/shard_map/while/body/eval_jaxpr/sij,scj->sic/dot_general | solution.py:88
  207.6 3.5 %fusion.223 = bf16[16,8,128,512]{3,2,1,0:T(8,128)(2,1)} fusion(bf16[16,8,128,512]{3,2,1,0:T(8,128)(2,1)} %get-tuple-element.249, s32[]{:T(128)} %get-tuple-element.248, f32[8,128]{1,0:T(8,128)S(1)} %add_convert_fusion.5, f32[8,512]{1,0:T(8,128)S(1)} %dynamic-slice_bitcast_fusion.4, bf16[16,8,128,128]{3,2,1,0:T(8,128)(2,1)} %get-tuple-element.260), kind=kOutput, calls=%fused_computation.13.clone.1 | convolution fusion | flops 144179200 | bytes 1332224 | tf_op jit(solution)/shard_map/while/body/eval_jaxpr/sij,scj->sic/dot_general | solution.py:88
  213.6 3.5 %fusion.223 = bf16[16,8,128,512]{3,2,1,0:T(8,128)(2,1)} fusion(bf16[16,8,128,512]{3,2,1,0:T(8,128)(2,1)} %get-tuple-element.249, s32[]{:T(128)} %get-tuple-element.248, f32[8,128]{1,0:T(8,128)S(1)} %add_convert_fusion.5, f32[8,512]{1,0:T(8,128)S(1)} %dynamic-slice_bitcast_fusion.4, bf16[16,8,128,128]{3,2,1,0:T(8,128)(2,1)} %get-tuple-element.260), kind=kOutput, calls=%fused_computation.13.clone.1 | convolution fusion | flops 144179200 | bytes 1332224 | tf_op jit(solution)/shard_map/while/body/eval_jaxpr/sij,scj->sic/dot_general | solution.py:88
  219.6 3.5 %fusion.223 = bf16[16,8,128,512]{3,2,1,0:T(8,128)(2,1)} fusion(bf16[16,8,128,512]{3,2,1,0:T(8,128)(2,1)} %get-tuple-element.249, s32[]{:T(128)} %get-tuple-element.248, f32[8,128]{1,0:T(8,128)S(1)} %add_convert_fusion.5, f32[8,512]{1,0:T(8,128)S(1)} %dynamic-slice_bitcast_fusion.4, bf16[16,8,128,128]{3,2,1,0:T(8,128)(2,1)} %get-tuple-element.260), kind=kOutput, calls=%fused_computation.13.clone.1 | convolution fusion | flops 144179200 | bytes 1332224 | tf_op jit(solution)/shard_map/while/body/eval_jaxpr/sij,scj->sic/dot_general | solution.py:88
  225.6 3.5 %fusion.223 = bf16[16,8,128,512]{3,2,1,0:T(8,128)(2,1)} fusion(bf16[16,8,128,512]{3,2,1,0:T(8,128)(2,1)} %get-tuple-element.249, s32[]{:T(128)} %get-tuple-element.248, f32[8,128]{1,0:T(8,128)S(1)} %add_convert_fusion.5, f32[8,512]{1,0:T(8,128)S(1)} %dynamic-slice_bitcast_fusion.4, bf16[16,8,128,128]{3,2,1,0:T(8,128)(2,1)} %get-tuple-element.260), kind=kOutput, calls=%fused_computation.13.clone.1 | convolution fusion | flops 144179200 | bytes 1332224 | tf_op jit(solution)/shard_map/while/body/eval_jaxpr/sij,scj->sic/dot_general | solution.py:88
  231.6 3.5 %fusion.223 = bf16[16,8,128,512]{3,2,1,0:T(8,128)(2,1)} fusion(bf16[16,8,128,512]{3,2,1,0:T(8,128)(2,1)} %get-tuple-element.249, s32[]{:T(128)} %get-tuple-element.248, f32[8,128]{1,0:T(8,128)S(1)} %add_convert_fusion.5, f32[8,512]{1,0:T(8,128)S(1)} %dynamic-slice_bitcast_fusion.4, bf16[16,8,128,128]{3,2,1,0:T(8,128)(2,1)} %get-tuple-element.260), kind=kOutput, calls=%fused_computation.13.clone.1 | convolution fusion | flops 144179200 | bytes 1332224 | tf_op jit(solution)/shard_map/while/body/eval_jaxpr/sij,scj->sic/dot_general | solution.py:88
  237.6 3.5 %fusion.223 = bf16[16,8,128,512]{3,2,1,0:T(8,128)(2,1)} fusion(bf16[16,8,128,512]{3,2,1,0:T(8,128)(2,1)} %get-tuple-element.249, s32[]{:T(128)} %get-tuple-element.248, f32[8,128]{1,0:T(8,128)S(1)} %add_convert_fusion.5, f32[8,512]{1,0:T(8,128)S(1)} %dynamic-slice_bitcast_fusion.4, bf16[16,8,128,128]{3,2,1,0:T(8,128)(2,1)} %get-tuple-element.260), kind=kOutput, calls=%fused_computation.13.clone.1 | convolution fusion | flops 144179200 | bytes 1332224 | tf_op jit(solution)/shard_map/while/body/eval_jaxpr/sij,scj->sic/dot_general | solution.py:88
  243.6 3.5 %fusion.223 = bf16[16,8,128,512]{3,2,1,0:T(8,128)(2,1)} fusion(bf16[16,8,128,512]{3,2,1,0:T(8,128)(2,1)} %get-tuple-element.249, s32[]{:T(128)} %get-tuple-element.248, f32[8,128]{1,0:T(8,128)S(1)} %add_convert_fusion.5, f32[8,512]{1,0:T(8,128)S(1)} %dynamic-slice_bitcast_fusion.4, bf16[16,8,128,128]{3,2,1,0:T(8,128)(2,1)} %get-tuple-element.260), kind=kOutput, calls=%fused_computation.13.clone.1 | convolution fusion | flops 144179200 | bytes 1332224 | tf_op jit(solution)/shard_map/while/body/eval_jaxpr/sij,scj->sic/dot_general | solution.py:88
  249.6 3.5 %fusion.223 = bf16[16,8,128,512]{3,2,1,0:T(8,128)(2,1)} fusion(bf16[16,8,128,512]{3,2,1,0:T(8,128)(2,1)} %get-tuple-element.249, s32[]{:T(128)} %get-tuple-element.248, f32[8,128]{1,0:T(8,128)S(1)} %add_convert_fusion.5, f32[8,512]{1,0:T(8,128)S(1)} %dynamic-slice_bitcast_fusion.4, bf16[16,8,128,128]{3,2,1,0:T(8,128)(2,1)} %get-tuple-element.260), kind=kOutput, calls=%fused_computation.13.clone.1 | convolution fusion | flops 144179200 | bytes 1332224 | tf_op jit(solution)/shard_map/while/body/eval_jaxpr/sij,scj->sic/dot_general | solution.py:88
  253.1 5.2 %fusion.87 = bf16[32,1024]{1,0:T(8,128)(2,1)S(1)} fusion(bf16[512,8,8,128]{3,2,1,0:T(8,128)(2,1)} %bitcast.208, f32[4096]{0:T(1024)S(1)} %mul.388, f32[4096]{0:T(1024)S(1)} %add_convert_fusion.2, f32[32]{0:T(128)S(1)} %add_multiply_fusion.1), kind=kOutput, calls=%fused_computation.106 | convolution fusion | flops 270958592 | bytes 8487040 | tf_op jit(solution)/shard_map/dot_general | solution.py:189
  260.6 3.4 %collective-permute-start.1 = (bf16[2,8,128]{2,1,0:T(8,128)(2,1)S(1)}, bf16[2,8,128]{2,1,0:T(8,128)(2,1)S(1)}, u32[]{:S(2)}, u32[]{:S(2)}) collective-permute-start(bf16[2,8,128]{2,1,0:T(8,128)(2,1)S(1)} %bitcast.206), channel_id=1, source_target_pairs={{2,0},{4,2},{6,4},{8,6},{10,8},{12,10},{14,12},{3,1},{5,3},{7,5},{... | collective-permute-start | bytes 12296 | tf_op jit(solution)/shard_map/ppermute | solution.py:24
  267.3 5.1 %collective-permute-start.3 = (bf16[36,8,2]{2,1,0:T(8,128)(2,1)S(1)}, bf16[36,8,2]{2,1,0:T(8,128)(2,1)S(1)}, u32[]{:S(2)}, u32[]{:S(2)}) collective-permute-start(bf16[36,8,2]{2,1,0:T(8,128)(2,1)S(1)} %get-tuple-element.160), channel_id=1, source_target_pairs={{1,0},{3,2},{5,4},{7,6},{9,8},{11,10},{13,12},{15,14},{17,16},{19,... | collective-permute-start | bytes 3464 | tf_op jit(solution)/shard_map/ppermute | solution.py:24
  278.3 3.3 %fusion.82 = f32[128,512,8]{1,2,0:T(8,128)S(1)} fusion(f32[128,8,512]{2,0,1:T(8,128)S(1)} %fusion.96, f32[8,8]{1,0:T(8,128)S(1)} %copy-done.2), kind=kOutput, calls=%fused_computation.102 | convolution fusion | flops 50331648 | bytes 4194560 | tf_op jit(solution)/shard_map/bk,rkc->brc/dot_general | solution.py:73
  281.6 5.2 %fusion.84 = f32[128,512]{1,0:T(8,128)S(1)} fusion(bf16[16384,512]{1,0:T(8,128)(2,1)S(1)} %bitcast.207, f32[16384]{0:T(1024)S(1)} %broadcast_bitcast_fusion, f32[16384]{0:T(1024)S(1)} %fusion.132, f32[128]{0:T(128)S(1)} %fusion.168, f32[1,128,512]{2,0,1:T(1,128)S(1)} %fusion.80), kind=kOutput, calls=%fused_computation.105 | convolution fusion | flops 2187395072 | bytes 17433088 | tf_op jit(solution)/shard_map/dot_general | solution.py:183
  (204 shorter events, 63.8 us)
Async XLA Ops:
  0.0 14.3 %copy-start = (bf16[64,128,128]{2,1,0:T(8,128)(2,1)S(1)}, bf16[64,128,128]{2,1,0:T(8,128)(2,1)}, u32[]{:S(2)}) copy-start(bf16[64,128,128]{2,1,0:T(8,128)(2,1)} %param.19) | copy-start | bytes 6291460
  8.7 51.4 %all-to-all-start.1 = ((bf16[8,16,32,256]{3,2,1,0:T(8,128)(2,1)}), bf16[8,16,32,256]{3,2,1,0:T(8,128)(2,1)}, u32[]{:S(2)}, u32[]{:S(2)}) async-start(bf16[8,16,32,256]{3,2,1,0:T(8,128)(2,1)} %select_select_fusion.1), calls=%async_computation.1 | async-start | bytes 4194304 | tf_op jit(solution)/shard_map/all_to_all | solution.py:163
  21.2 45.3 %copy-start.3 = (s32[3,128]{1,0:T(4,128)S(1)}, s32[3,128]{1,0:T(4,128)}, u32[]{:S(2)}) copy-start(s32[3,128]{1,0:T(4,128)} %param.22) | copy-start | bytes 4612
  21.2 45.8 %copy-start.8 = (u32[32]{0:T(128)S(1)}, u32[32]{0:T(128)}, u32[]{:S(2)}) copy-start(u32[32]{0:T(128)} %constant.385) | copy-start | bytes 388
  21.2 47.1 %copy-start.6 = (f32[1,8]{1,0:T(1,128)S(1)}, f32[1,8]{1,0:T(1,128)}, u32[]{:S(2)}) copy-start(f32[1,8]{1,0:T(1,128)} %param.24) | copy-start | bytes 100
  21.2 51.2 %copy-start.1 = (f32[3]{0:T(128)S(1)}, f32[3]{0:T(128)}, u32[]{:S(2)}) copy-start(f32[3]{0:T(128)} %param.23) | copy-start | bytes 40
  60.0 97.1 %all-to-all-start = ((bf16[8,16,128,128]{3,2,1,0:T(8,128)(2,1)}), bf16[8,16,128,128]{3,2,1,0:T(8,128)(2,1)}, u32[]{:S(2)}, u32[]{:S(2)}) async-start(bf16[8,16,128,128]{3,2,1,0:T(8,128)(2,1)} %select_select_fusion), calls=%async_computation | async-start | bytes 8388608 | tf_op jit(solution)/shard_map/all_to_all | solution.py:156
  253.1 28.6 %copy-start.7 = (bf16[16,8,128,512]{3,2,1,0:T(8,128)(2,1)S(1)}, bf16[16,8,128,512]{3,2,1,0:T(8,128)(2,1)}, u32[]{:S(2)}) copy-start(bf16[16,8,128,512]{3,2,1,0:T(8,128)(2,1)} %get-tuple-element.140) | copy-start | bytes 50331652
  258.3 5.7 %collective-permute-start = (bf16[2,8,128]{2,1,0:T(8,128)(2,1)S(1)}, bf16[2,8,128]{2,1,0:T(8,128)(2,1)S(1)}, u32[]{:S(2)}, u32[]{:S(2)}) collective-permute-start(bf16[2,8,128]{2,1,0:T(8,128)(2,1)S(1)} %bitcast.205), channel_id=1, source_target_pairs={{0,2},{2,4},{4,6},{6,8},{8,10},{10,12},{12,14},{1,3},{3,5},{5,7},{... | collective-permute-start | bytes 12296 | tf_op jit(solution)/shard_map/ppermute | solution.py:22
  260.6 5.3 %collective-permute-start.1 = (bf16[2,8,128]{2,1,0:T(8,128)(2,1)S(1)}, bf16[2,8,128]{2,1,0:T(8,128)(2,1)S(1)}, u32[]{:S(2)}, u32[]{:S(2)}) collective-permute-start(bf16[2,8,128]{2,1,0:T(8,128)(2,1)S(1)} %bitcast.206), channel_id=1, source_target_pairs={{2,0},{4,2},{6,4},{8,6},{10,8},{12,10},{14,12},{3,1},{5,3},{7,5},{... | collective-permute-start | bytes 12296 | tf_op jit(solution)/shard_map/ppermute | solution.py:24
  266.0 8.2 %collective-permute-start.2 = (bf16[36,8,2]{2,1,0:T(8,128)(2,1)S(1)}, bf16[36,8,2]{2,1,0:T(8,128)(2,1)S(1)}, u32[]{:S(2)}, u32[]{:S(2)}) collective-permute-start(bf16[36,8,2]{2,1,0:T(8,128)(2,1)S(1)} %get-tuple-element.159), channel_id=1, source_target_pairs={{0,1},{2,3},{4,5},{6,7},{8,9},{10,11},{12,13},{14,15},{16,17},{18,... | collective-permute-start | bytes 3464 | tf_op jit(solution)/shard_map/ppermute | solution.py:22
  267.3 6.9 %collective-permute-start.3 = (bf16[36,8,2]{2,1,0:T(8,128)(2,1)S(1)}, bf16[36,8,2]{2,1,0:T(8,128)(2,1)S(1)}, u32[]{:S(2)}, u32[]{:S(2)}) collective-permute-start(bf16[36,8,2]{2,1,0:T(8,128)(2,1)S(1)} %get-tuple-element.160), channel_id=1, source_target_pairs={{1,0},{3,2},{5,4},{7,6},{9,8},{11,10},{13,12},{15,14},{17,16},{19,... | collective-permute-start | bytes 3464 | tf_op jit(solution)/shard_map/ppermute | solution.py:24
  274.2 1.1 copy-start.4
  274.7 3.6 %copy-start.2 = (f32[8,8]{1,0:T(8,128)S(1)}, f32[8,8]{1,0:T(8,128)}, u32[]{:S(2)}) copy-start(f32[8,8]{1,0:T(8,128)} %param.25) | copy-start | bytes 772
  281.6 5.2 %copy-start.5 = (f32[8]{0:T(128)S(1)}, f32[8]{0:T(128)}, u32[]{:S(2)}) copy-start(f32[8]{0:T(128)} %param.26) | copy-start | bytes 100
where the time goes:
time: 294 us; the launch traced here: 289 us
  waiting for transfers between devices  102 us (35%)
  matrix products  92.2 us (31%)
  other arithmetic  36.2 us (12%)
  local copies, waits for them, and re-layouts  29.7 us (10%)
  starting transfers between devices  24.1 us (8%)
  blocking collectives  3.99 us (1%)
    all_to_all x1, waiting for transfers between devices, local(): lax.all_to_all(pan_send.reshape(row_owners, capacity, block_size, block_s...  60.9 us
    dot_general x16, matrix products, column_pass(): jnp.einsum('sij,scj->sic', pan_data, col_weight, preferred_element_type=j...  55.7 us
    all_to_all x1, waiting for transfers between devices, local(): lax.all_to_all(ms_send.reshape(row_owners, capacity, coarse_size, ms_bloc...  38.8 us
    dot_general x16, matrix products, column_pass(): jnp.einsum('sibj,scj->sibc', spread, ms_col_weight, preferred_element_typ...  18.8 us
    dynamic_slice x16, local copies, waits for them, and re-layouts, grouped_pass(): pan_cols, ms_cols = lax.map(column_pass, stacked)  14.6 us
    add x2, other arithmetic, along_nodes(): return left_node + (right_node - left_node) * within  12 us
    mul x1, other arithmetic, local(): x_ms = (along_nodes(band_nodes[0], coarse_pos, 0.5, GRID) - 1.5) * 0.25  10.1 us
    ppermute x2, starting transfers between devices, padded(): lax.ppermute(head, axis, [((i + 1) % count, i) for i in range(ends)])  8.42 us
  transfers between devices with their start and end apart: 6, of which 3 were waited for; matrix products, arithmetic and copies ran while one was open for 12% of the time, Pallas kernels for 0%

commit v1 on v0

v1 whole, which is shorter than its diff:
```python
import functools

import jax
import jax.numpy as jnp
from jax import lax
from jax.experimental import pallas as pl
from jax.experimental.pallas import tpu as pltpu
from jax.sharding import PartitionSpec as P

GRID = 64
TR = 128
TC = 512
KR = 2
KC = 5
MESH = pl.DeviceIdType.MESH
F32 = jnp.float32
BF16 = jnp.bfloat16


def cubic_weight(offset):
    distance = jnp.abs(offset)
    near_part = (1.5 * distance - 2.5) * distance * distance + 1.0
    far_part = ((-0.5 * distance + 2.5) * distance - 4.0) * distance + 2.0
    return jnp.where(
        distance <= 1.0, near_part, jnp.where(distance < 2.0, far_part, jnp.zeros_like(distance))
    )


def iota(shape, dim):
    return lax.broadcasted_iota(jnp.int32, shape, dim)


def cell_sums(capacity, send_ref, pan_ref, ms_ref, pan_out, ms_out, slot_block, pan_acc, ms_acc):
    tile = pl.program_id(0)
    own_blocks, block_size, _ = pan_ref.shape
    _, coarse_size, coarse_width = ms_ref.shape
    first_col = lax.axis_index("mcol") * KC

    @pl.when(tile == 0)
    def _():
        def clear(slot, carry):
            slot_block[slot] = -1
            return carry

        lax.fori_loop(0, slot_block.shape[0], clear, 0)

        def enter(block, carry):
            slot_block[send_ref[0, block]] = block
            return carry

        lax.fori_loop(0, own_blocks, enter, 0)

    pan_acc[...] = jnp.zeros_like(pan_acc)
    ms_acc[...] = jnp.zeros_like(ms_acc)

    def add(slot, carry):
        block = slot_block[tile * capacity + slot]

        @pl.when(block >= 0)
        def _():
            row = send_ref[1, block]
            col = send_ref[2, block] - first_col
            at = (
                pl.ds(pl.multiple_of(row * block_size, block_size), block_size),
                pl.ds(pl.multiple_of(col * block_size, block_size), block_size),
            )
            pan_acc[at] += pan_ref[block].astype(F32)
            at = (
                pl.ds(pl.multiple_of(row * coarse_size, coarse_size), coarse_size),
                pl.ds(pl.multiple_of(col * coarse_width, coarse_width), coarse_width),
            )
            ms_acc[at] += ms_ref[block].astype(F32)

        return carry

    lax.fori_loop(0, capacity, add, 0)
    pan_out[0] = pan_acc[...].astype(BF16)
    ms_out[0] = ms_acc[...].astype(BF16)


def row_coord(nodes, position, offset):
    first = position < GRID
    a = jnp.where(first, nodes[0:1, 0:1], nodes[0:1, 1:2])
    b = jnp.where(first, nodes[0:1, 1:2], nodes[0:1, 2:3])
    within = (jnp.where(first, position, position - GRID).astype(F32) + offset) / GRID
    return a + (b - a) * within


def col_coord(nodes, after, is_last, count, position, offset):
    segment = position // GRID
    coord = jnp.zeros(position.shape, F32)
    for s in range(count):
        left, shift = nodes[1:2, s : s + 1], s * GRID
        if s + 1 < count:
            right = nodes[1:2, s + 1 : s + 2]
        else:
            right = jnp.where(is_last, left, after)
            left = jnp.where(is_last, nodes[1:2, s - 1 : s], left)
            shift = jnp.where(is_last, shift - GRID, shift)
        within = ((position - shift).astype(F32) + offset) / GRID
        coord = jnp.where(segment == s, left + (right - left) * within, coord)
    return coord


def mapping(
    col_nodes,
    nodes_ref,
    pan_ref,
    ms_ref,
    mix_ref,
    gain_ref,
    out_ref,
    nodes_all,
    nodes_beside,
    pair_send,
    pair_recv,
    owner_send,
    owner_recv,
    total,
    col_weight,
    ms_col_weight,
    window,
    beside,
    up_cols,
    up_rows,
    pan_map,
    upsampled,
    nodes_ss,
    nodes_rs,
    pair_ss,
    pair_rs,
    owner_ss,
    owner_rs,
    halo_ss,
    halo_rs,
):
    n = lax.axis_size("mrow")
    pairs = n // 2
    scene = lax.axis_index("scene")
    m = lax.axis_index("mrow")
    c = lax.axis_index("mcol")
    z, y = m // 2, m % 2
    twin = z * 2 + (1 - y)
    other = 1 - c
    cols = pan_ref.shape[2]
    pan_rows = pan_ref.shape[1]
    ms_rows = ms_ref.shape[1]
    bands = out_ref.shape[0]
    coarse_rows = TR // 4
    coarse_cols = TC // 4
    half = coarse_rows // 2
    coarse_size = ms_rows // KR

    def at(row, col):
        return (scene, row, col)

    barrier = pltpu.get_barrier_semaphore()

    def greet(k, carry):
        row = lax.rem(m + k, n)
        pl.semaphore_signal(barrier, inc=1, device_id=at(row, c), device_id_type=MESH)
        pl.semaphore_signal(barrier, inc=1, device_id=at(row, other), device_id_type=MESH)
        return carry

    pl.semaphore_signal(barrier, inc=1, device_id=at(m, other), device_id_type=MESH)
    lax.fori_loop(1, n, greet, 0)
    pl.semaphore_wait(barrier, 2 * n - 1)

    def nodes_copy(slot, row):
        return pltpu.make_async_remote_copy(
            src_ref=nodes_ref,
            dst_ref=nodes_all.at[slot],
            send_sem=nodes_ss.at[row],
            recv_sem=nodes_rs.at[slot],
            device_id=at(row, c),
            device_id_type=MESH,
        )

    beside_copy = pltpu.make_async_remote_copy(
        src_ref=nodes_ref,
        dst_ref=nodes_beside,
        send_sem=nodes_ss.at[n],
        recv_sem=nodes_rs.at[n],
        device_id=at(m, other),
        device_id_type=MESH,
    )

    def send_nodes(k, carry):
        nodes_copy(m, lax.rem(m + k, n)).start()
        return carry

    lax.fori_loop(1, n, send_nodes, 0)
    beside_copy.start()
    nodes_all[m] = nodes_ref[...]

    tap = iota((TR, 2 * coarse_rows), 1) - (half - 2)
    spot = (iota((TR, 2 * coarse_rows), 0).astype(F32) - 1.5) * 0.25 + 2.0
    up_rows[...] = cubic_weight(spot - tap.astype(F32)).astype(BF16)
    spot = (iota((coarse_cols, TC), 1).astype(F32) - 1.5) * 0.25 + 2.0
    tap = iota((coarse_cols, TC), 0) + 2
    up_cols[0] = cubic_weight(spot - tap.astype(F32)).astype(BF16)
    tap = tap + jnp.where(c == 0, coarse_cols, -coarse_cols)
    up_cols[1] = cubic_weight(spot - tap.astype(F32)).astype(BF16)

    def wait_nodes(k, carry):
        row = lax.rem(m + k, n)
        nodes_copy(row, row).wait()
        return carry

    lax.fori_loop(1, n, wait_nodes, 0)
    beside_copy.wait()

    def row_pass(tile):
        nodes = nodes_all[tile]
        shape = (TR, pan_rows)
        weight = cubic_weight(
            row_coord(nodes, iota(shape, 0), 0.0) - iota(shape, 1).astype(F32)
        ).astype(BF16)
        pan = jnp.dot(weight, pan_ref[tile], preferred_element_type=F32)
        shape = (coarse_rows, ms_rows)
        spots = (row_coord(nodes, 4 * iota(shape, 0) + 1, 0.5) - 1.5) * 0.25
        weight = cubic_weight(spots - iota(shape, 1).astype(F32)).astype(BF16)
        left = jnp.dot(weight, ms_ref[tile, :, 0:cols], preferred_element_type=F32)
        right = jnp.dot(weight, ms_ref[tile, :, cols : 2 * cols], preferred_element_type=F32)
        return pan, left, right

    pieces = (
        slice(0, TR),
        slice(TR, TR + coarse_rows),
        slice(TR + coarse_rows, TR + 2 * coarse_rows),
    )

    def pair_copy(k):
        return pltpu.make_async_remote_copy(
            src_ref=pair_send.at[k],
            dst_ref=pair_recv.at[k],
            send_sem=pair_ss.at[k],
            recv_sem=pair_rs.at[k],
            device_id=at(twin, c),
            device_id_type=MESH,
        )

    def to_twin(k, carry):
        line = lax.rem(z + 1 + k, pairs)
        for part, value in zip(pieces, row_pass(line * 2 + 1 - y)):
            pair_send[k, part, :] = value.astype(BF16)
        pair_copy(k).start()
        return carry

    lax.fori_loop(0, pairs, to_twin, 0)

    own_nodes = nodes_ref[...]
    after = nodes_beside[1:2, 0:1]
    is_last = c == lax.axis_size("mcol") - 1
    x_pan = col_coord(own_nodes, after, is_last, col_nodes, iota((1, TC), 1), 0.0)
    for k in range(KC):
        size = cols // KC
        pixel = (c * KC + k) * size + iota((size, TC), 0)
        col_weight[k * size : (k + 1) * size, :] = cubic_weight(
            x_pan - pixel.astype(F32)
        ).astype(BF16)
    x_ms = col_coord(own_nodes, after, is_last, col_nodes, 4 * iota((1, coarse_cols), 1) + 1, 0.5)
    x_ms = (x_ms - 1.5) * 0.25
    ms_col_weight[...] = jnp.zeros_like(ms_col_weight)
    for k in range(KC):
        pixel = (c * KC + k) * coarse_size + iota((coarse_size, coarse_cols), 0)
        weight = cubic_weight(x_ms - pixel.astype(F32)).astype(BF16)
        for b in range(bands):
            row = (k * bands + b) * coarse_size
            ms_col_weight[row : row + coarse_size, b * coarse_cols : (b + 1) * coarse_cols] = weight

    def owner_copy(k, line, slot):
        return pltpu.make_async_remote_copy(
            src_ref=owner_send.at[k],
            dst_ref=owner_recv.at[slot],
            send_sem=owner_ss.at[k],
            recv_sem=owner_rs.at[slot],
            device_id=at(line * 2 + y, c),
            device_id_type=MESH,
        )

    def to_owner(k, carry):
        line = lax.rem(z + 1 + k, pairs)
        values = row_pass(line * 2 + y)
        pair_copy(k).wait()
        for part, value in zip(pieces, values):
            owner_send[k, part, :] = (value + pair_recv[k, part, :].astype(F32)).astype(BF16)
        owner_copy(k, line, z).start()
        return carry

    lax.fori_loop(0, pairs - 1, to_owner, 0)
    values = row_pass(m)
    pair_copy(pairs - 1).wait()
    for part, value in zip(pieces, values):
        total[part, :] = value + pair_recv[pairs - 1, part, :].astype(F32)

    def from_line(k, carry):
        line = lax.rem(z + pairs - 1 - k, pairs)
        owner_copy(k, line, line).wait()
        total[...] += owner_recv[line].astype(F32)
        return carry

    lax.fori_loop(0, pairs - 1, from_line, 0)

    ms_sum = [total[part, :].astype(BF16) for part in pieces[1:]]
    ms_map = jnp.dot(ms_sum[0], ms_col_weight[0:cols, :], preferred_element_type=F32)
    ms_map = ms_map + jnp.dot(
        ms_sum[1], ms_col_weight[cols : 2 * cols, :], preferred_element_type=F32
    )
    window[half : half + coarse_rows, :] = ms_map.astype(BF16)

    has_above, has_below = m > 0, m < n - 1

    def halo_copy(k, src, dst, row, col):
        return pltpu.make_async_remote_copy(
            src_ref=window.at[pl.ds(src, half)] if k else window.at[pl.ds(src, coarse_rows)],
            dst_ref=dst,
            send_sem=halo_ss.at[k],
            recv_sem=halo_rs.at[k],
            device_id=at(row, col),
            device_id_type=MESH,
        )

    mid = half + coarse_rows
    across_copy = halo_copy(0, half, beside.at[pl.ds(half, coarse_rows)], m, other)
    up_copies = [
        halo_copy(1, half, window.at[pl.ds(mid, half)], m - 1, c),
        halo_copy(2, half, beside.at[pl.ds(mid, half)], m - 1, other),
    ]
    down_copies = [
        halo_copy(3, coarse_rows, window.at[pl.ds(0, half)], m + 1, c),
        halo_copy(4, coarse_rows, beside.at[pl.ds(0, half)], m + 1, other),
    ]
    across_copy.start()

    @pl.when(has_above)
    def _():
        for copy in up_copies:
            copy.start()

    @pl.when(has_below)
    def _():
        for copy in down_copies:
            copy.start()

    pan_map[...] = jnp.dot(
        total[pieces[0], :].astype(BF16), col_weight[...], preferred_element_type=F32
    )

    across_copy.wait()

    @pl.when(has_above)
    def _():
        for copy in up_copies:
            copy.wait_send()
        for copy in down_copies:
            copy.wait_recv()

    @pl.when(has_below)
    def _():
        for copy in down_copies:
            copy.wait_send()
        for copy in up_copies:
            copy.wait_recv()

    @pl.when(jnp.logical_not(has_above))
    def _():
        window[0:half, :] = jnp.zeros((half, window.shape[1]), BF16)
        beside[0:half, :] = jnp.zeros((half, window.shape[1]), BF16)

    @pl.when(jnp.logical_not(has_below))
    def _():
        window[mid : mid + half, :] = jnp.zeros((half, window.shape[1]), BF16)
        beside[mid : mid + half, :] = jnp.zeros((half, window.shape[1]), BF16)

    for b in range(bands):
        lanes = slice(b * coarse_cols, (b + 1) * coarse_cols)
        across = jnp.dot(window[:, lanes], up_cols[0], preferred_element_type=F32)
        across = across + jnp.dot(beside[:, lanes], up_cols[1], preferred_element_type=F32)
        upsampled[b] = jnp.dot(up_rows[...], across.astype(BF16), preferred_element_type=F32)

    def combine(k, carry):
        rows = pl.ds(pl.multiple_of(k * 16, 16), 16)
        for lane in range(0, TC, 128):
            values = [upsampled[b, rows, lane : lane + 128] for b in range(bands)]
            pan = pan_map[rows, lane : lane + 128]
            for b in range(bands):
                mixed = gain_ref[b] * pan
                for other_band in range(bands):
                    mixed = mixed + mix_ref[b, other_band] * values[other_band]
                out_ref[b, rows, lane : lane + 128] = mixed.astype(BF16)
        return carry

    lax.fori_loop(0, TR // 16, combine, 0)


def local(
    pan_blocks,
    ms_blocks,
    send_list,
    tile_list,
    row_grid,
    col_grid,
    band_mix,
    band_gain,
    synth_weight,
):
    n = lax.axis_size("mrow")
    pairs = n // 2
    own_blocks, block_size, _ = pan_blocks.shape
    _, coarse_size, coarse_width = ms_blocks.shape
    slots = tile_list.shape[1]
    capacity = slots // n
    bands = band_gain.shape[0]
    pan_rows, pan_cols = KR * block_size, KC * block_size
    ms_rows, ms_cols = KR * coarse_size, KC * coarse_width
    smem = pl.BlockSpec(memory_space=pltpu.SMEM)
    vmem = pl.BlockSpec(memory_space=pltpu.VMEM)
    pan_cells, ms_cells = pl.pallas_call(
        functools.partial(cell_sums, capacity),
        grid=(n,),
        out_shape=(
            jax.ShapeDtypeStruct((n, pan_rows, pan_cols), BF16),
            jax.ShapeDtypeStruct((n, ms_rows, ms_cols), BF16),
        ),
        in_specs=[smem, vmem, vmem],
        out_specs=(
            pl.BlockSpec((1, pan_rows, pan_cols), lambda t: (t, 0, 0)),
            pl.BlockSpec((1, ms_rows, ms_cols), lambda t: (t, 0, 0)),
        ),
        scratch_shapes=[
            pltpu.SMEM((slots,), jnp.int32),
            pltpu.VMEM((pan_rows, pan_cols), F32),
            pltpu.VMEM((ms_rows, ms_cols), F32),
        ],
        name="cell_sums",
    )(send_list, pan_blocks, ms_blocks)

    nodes = jnp.concatenate(
        [
            jnp.pad(row_grid[None, :], ((0, 0), (0, 128 - row_grid.shape[0]))),
            jnp.pad(col_grid, ((0, 6), (0, 128 - col_grid.shape[1]))),
        ],
        axis=0,
    )
    mix = jnp.eye(bands, dtype=F32) + band_mix - band_gain[:, None] * synth_weight[None, :]
    coarse_rows, coarse_cols = TR // 4, TC // 4
    piece_rows = TR + 2 * coarse_rows
    dma = pltpu.SemaphoreType.DMA
    return pl.pallas_call(
        functools.partial(mapping, col_grid.shape[1]),
        out_shape=jax.ShapeDtypeStruct((bands, TR, TC), BF16),
        in_specs=[vmem, vmem, vmem, smem, smem],
        out_specs=vmem,
        scratch_shapes=[
            pltpu.VMEM((n, 8, 128), F32),
            pltpu.VMEM((8, 128), F32),
            pltpu.VMEM((pairs, piece_rows, pan_cols), BF16),
            pltpu.VMEM((pairs, piece_rows, pan_cols), BF16),
            pltpu.VMEM((pairs, piece_rows, pan_cols), BF16),
            pltpu.VMEM((pairs, piece_rows, pan_cols), BF16),
            pltpu.VMEM((piece_rows, pan_cols), F32),
            pltpu.VMEM((pan_cols, TC), BF16),
            pltpu.VMEM((ms_cols, bands * coarse_cols), BF16),
            pltpu.VMEM((2 * coarse_rows, bands * coarse_cols), BF16),
            pltpu.VMEM((2 * coarse_rows, bands * coarse_cols), BF16),
            pltpu.VMEM((2, coarse_cols, TC), BF16),
            pltpu.VMEM((TR, 2 * coarse_rows), BF16),
            pltpu.VMEM((TR, TC), F32),
            pltpu.VMEM((bands, TR, TC), F32),
            dma((n + 1,)),
            dma((n + 1,)),
            dma((pairs,)),
            dma((pairs,)),
            dma((pairs,)),
            dma((pairs,)),
            dma((5,)),
            dma((5,)),
        ],
        compiler_params=pltpu.CompilerParams(
            collective_id=0, has_side_effects=True, vmem_limit_bytes=60 * 1024 * 1024
        ),
        name="mapping",
    )(nodes, pan_cells, ms_cells, mix, band_gain)


def solution(mesh):
    return jax.shard_map(
        local,
        mesh=mesh,
        in_specs=(
            P(("scene", "mrow", "mcol"), None, None),
            P(("scene", "mrow", "mcol"), None, None),
            P(None, ("scene", "mrow", "mcol")),
            P(None, ("scene", "mrow", "mcol")),
            P(("scene", "mrow")),
            P(("scene", "mrow"), "mcol"),
            P(),
            P(),
            P(),
        ),
        out_specs=P(None, ("scene", "mrow"), "mcol"),
        check_vma=False,
    )
```

time: 294 us -> 63.3 us (0.22); the launches traced: 289 us -> 62.2 us
  waiting for transfers between devices: 102 us -> 0 us
  matrix products: 92.2 us -> 0 us
  Pallas kernels: 0 us -> 57.3 us
  other arithmetic: 36.2 us -> 2.64 us
  local copies, waits for them, and re-layouts: 29.7 us -> 2.26 us
  starting transfers between devices: 24.1 us -> 0 us
  blocking collectives: 3.99 us -> 0 us
    all_to_all x2 -> x0, waiting for transfers between devices: 99.7 us -> none  [the longest x1 60.9 us: local(): lax.all_to_all(pan_send.reshape(row_owners, capacity, block_size, block_s...]
    dot_general x38 -> x0, matrix products: 92.2 us -> none  [the longest x16 55.7 us: column_pass(): jnp.einsum('sij,scj->sic', pan_data, col_weight, preferred_element_type=j...]
    pallas_call x0 -> x2, Pallas kernels: none -> 57.3 us  [the longest x1 48.4 us: local(): pl.pallas_call(functools.partial(mapping, col_grid.shape[1]), out_shape=j...]
    dynamic_slice x16 -> x0, local copies, waits for them, and re-layouts: 14.6 us -> none  [grouped_pass(): pan_cols, ms_cols = lax.map(column_pass, stacked)]
    mul x19 -> x0, other arithmetic: 12.1 us -> none  [the longest x1 10.1 us: local(): x_ms = (along_nodes(band_nodes[0], coarse_pos, 0.5, GRID) - 1.5) * 0.25]
    all_to_all x2 -> x0, starting transfers between devices: 12.1 us -> none  [the longest x1 6.45 us: local(): lax.all_to_all(pan_send.reshape(row_owners, capacity, block_size, block_s...]
    ppermute x4 -> x0, starting transfers between devices: 12 us -> none  [the longest x2 8.42 us: padded(): lax.ppermute(head, axis, [((i + 1) % count, i) for i in range(ends)])]
    add x4 -> x0, other arithmetic: 12 us -> none  [the longest x2 12 us: along_nodes(): return left_node + (right_node - left_node) * within]
  transfers between devices with their start and end apart: 6 -> 0, of which waited for: 3 -> 0; matrix products, arithmetic and copies ran while one was open for 12% -> 0% of each run, Pallas kernels for 0% -> 0%
where the time goes in v1:
time: 63.3 us; the launch traced here: 62.2 us
  Pallas kernels  57.3 us (91%)
  other arithmetic  2.64 us (4%)
  local copies, waits for them, and re-layouts  2.26 us (4%)
    pallas_call x1, Pallas kernels, local(): pl.pallas_call(functools.partial(mapping, col_grid.shape[1]), out_shape=j...  48.4 us
    pallas_call x1, Pallas kernels, local(): pl.pallas_call(functools.partial(cell_sums, capacity), grid=(n,), out_sha...  8.88 us
    unnamed x1, local copies, waits for them, and re-layouts  2.26 us
    sub x1, other arithmetic, local(): jnp.eye(bands, dtype=F32) + band_mix  1.37 us
    concatenate x1, other arithmetic, local(): jnp.concatenate([jnp.pad(row_grid[None, :], ((0, 0), (0, 128 - row_grid.s...  1.27 us

profile of v1, /device:TPU:15, one launch (start us, length us, event | category | flops | bytes accessed | tf_op | source)
XLA Modules:
  0.0 62.2 jit_solution(7298239549287488342)
XLA Ops:
  0.0 1.3 %select_maximum_fusion.nodes_ref = f32[8,128]{1,0:T(8,128)} fusion(f32[1,8]{1,0:T(1,128)} %param.13, f32[1,3]{1,0:T(1,128)} %bitcast.1), kind=kLoop, calls=%fused_computation | loop fusion | flops 5120 | bytes 4140 | tf_op jit(solution)/shard_map/concatenate | solution.py:439
  1.3 1.4 %multiply_subtract_fusion.mix_ref = f32[8,8]{1,0:T(8,128)} fusion(f32[8,8]{1,0:T(8,128)} %param.14, f32[8]{0:T(128)} %param.16, f32[8]{0:T(128)} %gain_ref.1), kind=kLoop, calls=%fused_computation.3 | loop fusion | flops 320 | bytes 576 | tf_op jit(solution)/shard_map/sub | solution.py:446
  2.6 8.9 %cell_sums.1 = (bf16[8,256,640]{2,1,0:T(8,128)(2,1)}, bf16[8,64,1280]{2,1,0:T(8,128)(2,1)}) custom-call(s32[3,64]{1,0:T(4,128)} %send_ref.1, bf16[64,128,128]{2,1,0:T(8,128)(2,1)} %pan_ref.1, bf16[64,32,256]{2,1,0:T(8,128)(2,1)} %ms_ref.1), custom_call_target="tpu_custom_call" | custom-call | tf_op jit(solution)/shard_map/cell_sums/pallas_call | solution.py:419
  11.5 48.4 %mapping.1 = bf16[8,128,512]{2,1,0:T(8,128)(2,1)} custom-call(f32[8,128]{1,0:T(8,128)} %select_maximum_fusion.nodes_ref, bf16[8,256,640]{2,1,0:T(8,128)(2,1)} %get-tuple-element.7.pan_ref, bf16[8,64,1280]{2,1,0:T(8,128)(2,1)} %get-tuple-element.8.ms_ref, f32[8,8]{1,0:T(8,128)} %multiply_subtract_fusion.mix_ref, f32[8]{0:T(128)} %gain_ref.1), custom_call_target="tpu_custom_call" | custom-call | tf_op jit(solution)/shard_map/mapping/pallas_call | solution.py:450
  59.9 2.3 %copy.10 = bf16[8,128,512]{2,1,0:T(8,128)(2,1)} copy(bf16[8,128,512]{2,1,0:T(8,128)(2,1)} %mapping.1) | data formatting | bytes 2097152

commit v2 on v1

v2 whole, which is shorter than its diff:
```python
import functools

import jax
import jax.numpy as jnp
from jax import lax
from jax.experimental import pallas as pl
from jax.experimental.pallas import tpu as pltpu
from jax.sharding import PartitionSpec as P

GRID = 64
TR = 128
TC = 512
KR = 2
KC = 5
MESH = pl.DeviceIdType.MESH
F32 = jnp.float32
BF16 = jnp.bfloat16


def cubic_weight(offset):
    outer = jnp.maximum(2.0 - jnp.abs(offset), 0.0)
    shifted = outer - 1.0
    inner = jnp.maximum(shifted, 0.0)
    return outer * outer * (0.5 * shifted) + inner * inner * (1.0 - 2.0 * inner)


def iota(shape, dim):
    return lax.broadcasted_iota(jnp.int32, shape, dim)


def cell_sums(
    capacity,
    send_ref,
    pan_ref,
    ms_ref,
    row_ref,
    col_ref,
    pan_out,
    ms_out,
    nodes_out,
    slot_block,
    pan_acc,
    ms_acc,
):
    tile = pl.program_id(0)
    own_blocks, block_size, _ = pan_ref.shape
    _, coarse_size, coarse_width = ms_ref.shape
    first_col = lax.axis_index("mcol") * KC

    @pl.when(tile == 0)
    def _():
        nodes_out[...] = jnp.zeros_like(nodes_out)
        nodes_out[0:1, 0 : row_ref.shape[1]] = row_ref[...]
        nodes_out[1:2, 0 : col_ref.shape[1]] = col_ref[...]

        def clear(slot, carry):
            slot_block[slot] = -1
            return carry

        lax.fori_loop(0, slot_block.shape[0], clear, 0)

        def enter(block, carry):
            slot_block[send_ref[0, block]] = block
            return carry

        lax.fori_loop(0, own_blocks, enter, 0)

    pan_acc[...] = jnp.zeros_like(pan_acc)
    ms_acc[...] = jnp.zeros_like(ms_acc)

    def add(slot, carry):
        block = slot_block[tile * capacity + slot]

        @pl.when(block >= 0)
        def _():
            row = send_ref[1, block]
            col = send_ref[2, block] - first_col
            at = (
                pl.ds(pl.multiple_of(row * block_size, block_size), block_size),
                pl.ds(pl.multiple_of(col * block_size, block_size), block_size),
            )
            pan_acc[at] += pan_ref[block].astype(F32)
            at = (
                pl.ds(pl.multiple_of(row * coarse_size, coarse_size), coarse_size),
                pl.ds(pl.multiple_of(col * coarse_width, coarse_width), coarse_width),
            )
            ms_acc[at] += ms_ref[block].astype(F32)

        return carry

    lax.fori_loop(0, capacity, add, 0)
    pan_out[0] = pan_acc[...].astype(BF16)
    ms_out[0] = ms_acc[...].astype(BF16)


def row_coord(nodes, position, offset):
    first = position < GRID
    a = jnp.where(first, nodes[0:1, 0:1], nodes[0:1, 1:2])
    b = jnp.where(first, nodes[0:1, 1:2], nodes[0:1, 2:3])
    within = (jnp.where(first, position, position - GRID).astype(F32) + offset) / GRID
    return a + (b - a) * within


def col_coord(nodes, after, is_last, count, position, offset):
    segment = position // GRID
    coord = jnp.zeros(position.shape, F32)
    for s in range(count):
        left, shift = nodes[1:2, s : s + 1], s * GRID
        if s + 1 < count:
            right = nodes[1:2, s + 1 : s + 2]
        else:
            right = jnp.where(is_last, left, after)
            left = jnp.where(is_last, nodes[1:2, s - 1 : s], left)
            shift = jnp.where(is_last, shift - GRID, shift)
        within = ((position - shift).astype(F32) + offset) / GRID
        coord = jnp.where(segment == s, left + (right - left) * within, coord)
    return coord


def mapping(
    col_nodes,
    nodes_ref,
    pan_hbm,
    ms_hbm,
    mix_ref,
    gain_ref,
    synth_ref,
    mixed_hbm,
    pan_map,
    pan_ref,
    ms_ref,
    nodes_all,
    ms_pair_send,
    ms_pair_recv,
    ms_owner_send,
    ms_owner_recv,
    pan_pair_send,
    pan_pair_recv,
    pan_owner_send,
    pan_owner_recv,
    ms_total,
    col_weight,
    ms_col_weight,
    window,
    beside,
    up_cols,
    up_rows,
    upsampled,
    mixed,
    load_sem,
    nodes_ss,
    nodes_rs,
    ms_pair_ss,
    ms_pair_rs,
    ms_owner_ss,
    ms_owner_rs,
    pan_pair_ss,
    pan_pair_rs,
    pan_owner_ss,
    pan_owner_rs,
    halo_ss,
    halo_rs,
):
    n = lax.axis_size("mrow")
    pairs = n // 2
    scene = lax.axis_index("scene")
    m = lax.axis_index("mrow")
    c = lax.axis_index("mcol")
    z, y = m // 2, m % 2
    twin = z * 2 + (1 - y)
    other = 1 - c
    cols = pan_ref.shape[2]
    pan_rows = pan_ref.shape[1]
    ms_rows = ms_ref.shape[1]
    bands = mixed.shape[0]
    coarse_rows = TR // 4
    coarse_cols = TC // 4
    half = coarse_rows // 2
    mid = half + coarse_rows
    coarse_size = ms_rows // KR
    is_last = c == lax.axis_size("mcol") - 1

    def at(row, col):
        return (scene, row, col)

    def line_of(k):
        return lax.rem(z + 1 + lax.rem(pairs // 2 - 1 + k, pairs - 1), pairs)

    barrier = pltpu.get_barrier_semaphore()

    def greet(k, carry):
        row = lax.rem(m + k, n)
        pl.semaphore_signal(barrier, inc=1, device_id=at(row, c), device_id_type=MESH)
        pl.semaphore_signal(barrier, inc=1, device_id=at(row, other), device_id_type=MESH)
        return carry

    pl.semaphore_signal(barrier, inc=1, device_id=at(m, other), device_id_type=MESH)
    lax.fori_loop(1, n, greet, 0)
    ms_load = pltpu.make_async_copy(ms_hbm, ms_ref, load_sem.at[0])
    pan_load = pltpu.make_async_copy(pan_hbm, pan_ref, load_sem.at[1])
    ms_load.start()
    pan_load.start()

    tap = iota((TR, 2 * coarse_rows), 1) - (half - 2)
    spot = (iota((TR, 2 * coarse_rows), 0).astype(F32) - 1.5) * 0.25 + 2.0
    up_rows[...] = cubic_weight(spot - tap.astype(F32)).astype(BF16)
    ms_col_weight[...] = jnp.zeros_like(ms_col_weight)
    pl.semaphore_wait(barrier, 2 * n - 1)

    def nodes_copy(slot_row, slot_col, row, col):
        return pltpu.make_async_remote_copy(
            src_ref=nodes_ref,
            dst_ref=nodes_all.at[slot_col, slot_row],
            send_sem=nodes_ss.at[col, row],
            recv_sem=nodes_rs.at[slot_col, slot_row],
            device_id=at(row, col),
            device_id_type=MESH,
        )

    def send_nodes(k, carry):
        row = lax.rem(m + k, n)
        nodes_copy(m, c, row, c).start()
        nodes_copy(m, c, row, other).start()
        return carry

    lax.fori_loop(1, n, send_nodes, 0)
    nodes_copy(m, c, m, other).start()
    nodes_all[c, m] = nodes_ref[...]

    spot = (iota((coarse_cols, TC), 1).astype(F32) - 1.5) * 0.25 + 2.0
    tap = iota((coarse_cols, TC), 0) + 2
    up_cols[0] = cubic_weight(spot - tap.astype(F32)).astype(BF16)
    tap = tap + jnp.where(c == 0, coarse_cols, -coarse_cols)
    up_cols[1] = cubic_weight(spot - tap.astype(F32)).astype(BF16)
    ms_load.wait()

    def wait_nodes(k, carry):
        row = lax.rem(m + k, n)
        nodes_copy(row, c, row, c).wait()
        nodes_copy(row, other, row, other).wait()
        return carry

    lax.fori_loop(1, n, wait_nodes, 0)
    nodes_copy(m, other, m, other).wait()

    sides = (slice(0, coarse_rows), slice(coarse_rows, 2 * coarse_rows))

    def ms_part(tile):
        nodes = nodes_all[c, tile]
        shape = (coarse_rows, ms_rows)
        spots = (row_coord(nodes, 4 * iota(shape, 0) + 1, 0.5) - 1.5) * 0.25
        weight = cubic_weight(spots - iota(shape, 1).astype(F32)).astype(BF16)
        left = jnp.dot(weight, ms_ref[tile, :, 0:cols], preferred_element_type=F32)
        right = jnp.dot(weight, ms_ref[tile, :, cols : 2 * cols], preferred_element_type=F32)
        return left, right

    def pan_part(tile):
        nodes = nodes_all[c, tile]
        after = nodes_all[1, tile][1:2, 0:1]
        x_pan = col_coord(nodes, after, is_last, col_nodes, iota((1, TC), 1), 0.0)
        size = cols // KC
        for k in range(KC):
            pixel = (c * KC + k) * size + iota((size, TC), 0)
            col_weight[k * size : (k + 1) * size, :] = cubic_weight(
                x_pan - pixel.astype(F32)
            ).astype(BF16)
        shape = (TR, pan_rows)
        weight = cubic_weight(
            row_coord(nodes, iota(shape, 0), 0.0) - iota(shape, 1).astype(F32)
        ).astype(BF16)
        rows = jnp.dot(weight, pan_ref[tile], preferred_element_type=F32)
        return jnp.dot(rows.astype(BF16), col_weight[...], preferred_element_type=F32)

    def pair_copy(send, recv, ss, rs, k):
        return pltpu.make_async_remote_copy(
            src_ref=send.at[k],
            dst_ref=recv.at[k],
            send_sem=ss.at[k],
            recv_sem=rs.at[k],
            device_id=at(twin, c),
            device_id_type=MESH,
        )

    def owner_copy(send, recv, ss, rs, k, line, slot):
        return pltpu.make_async_remote_copy(
            src_ref=send.at[k],
            dst_ref=recv.at[slot],
            send_sem=ss.at[k],
            recv_sem=rs.at[slot],
            device_id=at(line * 2 + y, c),
            device_id_type=MESH,
        )

    ms_pair = functools.partial(pair_copy, ms_pair_send, ms_pair_recv, ms_pair_ss, ms_pair_rs)
    pan_pair = functools.partial(pair_copy, pan_pair_send, pan_pair_recv, pan_pair_ss, pan_pair_rs)
    ms_owner = functools.partial(
        owner_copy, ms_owner_send, ms_owner_recv, ms_owner_ss, ms_owner_rs
    )
    pan_owner = functools.partial(
        owner_copy, pan_owner_send, pan_owner_recv, pan_owner_ss, pan_owner_rs
    )

    def ms_to_twin(k, tile):
        for side, value in zip(sides, ms_part(tile)):
            ms_pair_send[k, side, :] = value.astype(BF16)
        ms_pair(k).start()

    def pan_to_twin(k, tile):
        pan_pair_send[k] = pan_part(tile).astype(BF16)
        pan_pair(k).start()

    def each_line(first, last, step):
        def body(k, carry):
            step(k, line_of(k))
            return carry

        lax.fori_loop(first, last, body, 0)

    each_line(0, pairs - 1, lambda k, line: ms_to_twin(k, line * 2 + 1 - y))
    ms_to_twin(pairs - 1, twin)
    pan_load.wait()
    each_line(0, pairs - 1, lambda k, line: pan_to_twin(k, line * 2 + 1 - y))
    pan_to_twin(pairs - 1, twin)

    def ms_to_owner(k, line):
        values = ms_part(line * 2 + y)
        ms_pair(k).wait()
        for side, value in zip(sides, values):
            ms_owner_send[k, side, :] = (value + ms_pair_recv[k, side, :].astype(F32)).astype(BF16)
        ms_owner(k, line, z).start()

    each_line(0, pairs - 1, ms_to_owner)
    values = ms_part(m)
    ms_pair(pairs - 1).wait()
    for side, value in zip(sides, values):
        ms_total[side, :] = value + ms_pair_recv[pairs - 1, side, :].astype(F32)

    x_ms = col_coord(
        nodes_ref[...],
        nodes_all[1, m][1:2, 0:1],
        is_last,
        col_nodes,
        4 * iota((1, coarse_cols), 1) + 1,
        0.5,
    )
    x_ms = (x_ms - 1.5) * 0.25
    for k in range(KC):
        pixel = (c * KC + k) * coarse_size + iota((coarse_size, coarse_cols), 0)
        weight = cubic_weight(x_ms - pixel.astype(F32)).astype(BF16)
        for b in range(bands):
            row = (k * bands + b) * coarse_size
            ms_col_weight[row : row + coarse_size, b * coarse_cols : (b + 1) * coarse_cols] = weight

    def pan_to_owner(k, line):
        value = pan_part(line * 2 + y)
        pan_pair(k).wait()
        pan_owner_send[k] = (value + pan_pair_recv[k].astype(F32)).astype(BF16)
        pan_owner(k, line, z).start()

    each_line(0, pairs - 2, pan_to_owner)

    def ms_from_line(k, line):
        ms_owner(k, line, line).wait()
        ms_total[...] += ms_owner_recv[line].astype(F32)

    each_line(0, pairs - 1, ms_from_line)
    left, right = [ms_total[side, :].astype(BF16) for side in sides]
    ms_map = jnp.dot(left, ms_col_weight[0:cols, :], preferred_element_type=F32)
    ms_map = ms_map + jnp.dot(
        right, ms_col_weight[cols : 2 * cols, :], preferred_element_type=F32
    )
    window[half:mid, :] = ms_map.astype(BF16)

    has_above, has_below = m > 0, m < n - 1

    def halo_copy(k, src, rows, dst, start, row, col):
        return pltpu.make_async_remote_copy(
            src_ref=window.at[pl.ds(src, rows)],
            dst_ref=dst.at[pl.ds(start, rows)],
            send_sem=halo_ss.at[k],
            recv_sem=halo_rs.at[k],
            device_id=at(row, col),
            device_id_type=MESH,
        )

    across_copy = halo_copy(0, half, coarse_rows, beside, half, m, other)
    up_copies = [
        halo_copy(1, half, half, window, mid, m - 1, c),
        halo_copy(2, half, half, beside, mid, m - 1, other),
    ]
    down_copies = [
        halo_copy(3, coarse_rows, half, window, 0, m + 1, c),
        halo_copy(4, coarse_rows, half, beside, 0, m + 1, other),
    ]
    across_copy.start()

    @pl.when(has_above)
    def _():
        for copy in up_copies:
            copy.start()

    @pl.when(has_below)
    def _():
        for copy in down_copies:
            copy.start()

    pan_to_owner(pairs - 2, line_of(pairs - 2))
    pan_map[...] = pan_part(m)
    across_copy.wait()

    @pl.when(has_above)
    def _():
        for copy in up_copies:
            copy.wait_send()
        for copy in down_copies:
            copy.wait_recv()

    @pl.when(has_below)
    def _():
        for copy in down_copies:
            copy.wait_send()
        for copy in up_copies:
            copy.wait_recv()

    edge = jnp.zeros((half, window.shape[1]), BF16)

    @pl.when(jnp.logical_not(has_above))
    def _():
        window[0:half, :] = edge
        beside[0:half, :] = edge

    @pl.when(jnp.logical_not(has_below))
    def _():
        window[mid : mid + half, :] = edge
        beside[mid : mid + half, :] = edge

    for b in range(bands):
        lanes = slice(b * coarse_cols, (b + 1) * coarse_cols)
        across = jnp.dot(window[:, lanes], up_cols[0], preferred_element_type=F32)
        across = across + jnp.dot(beside[:, lanes], up_cols[1], preferred_element_type=F32)
        upsampled[b] = jnp.dot(up_rows[...], across.astype(BF16), preferred_element_type=F32)

    def mix_bands(k, carry):
        rows = pl.ds(pl.multiple_of(k * 16, 16), 16)
        for lane in range(0, TC, 128):
            values = [upsampled[b, rows, lane : lane + 128] for b in range(bands)]
            synthetic = sum(synth_ref[b] * values[b] for b in range(bands))
            for b in range(bands):
                result = values[b] - gain_ref[b] * synthetic
                for k2 in range(bands):
                    result = result + mix_ref[b, k2] * values[k2]
                mixed[b, rows, lane : lane + 128] = result.astype(BF16)
        return carry

    lax.fori_loop(0, TR // 16, mix_bands, 0)
    store = pltpu.make_async_copy(mixed, mixed_hbm, load_sem.at[2])
    store.start()

    pan_pair(pairs - 1).wait()
    pan_map[...] += pan_pair_recv[pairs - 1].astype(F32)

    def pan_from_line(k, line):
        pan_owner(k, line, line).wait()
        pan_map[...] += pan_owner_recv[line].astype(F32)

    each_line(0, pairs - 1, pan_from_line)
    store.wait()


def local(
    pan_blocks,
    ms_blocks,
    send_list,
    tile_list,
    row_grid,
    col_grid,
    band_mix,
    band_gain,
    synth_weight,
):
    n = lax.axis_size("mrow")
    pairs = n // 2
    own_blocks, block_size, _ = pan_blocks.shape
    _, coarse_size, coarse_width = ms_blocks.shape
    slots = tile_list.shape[1]
    capacity = slots // n
    bands = band_gain.shape[0]
    pan_rows, pan_cols = KR * block_size, KC * block_size
    ms_rows, ms_cols = KR * coarse_size, KC * coarse_width
    smem = pl.BlockSpec(memory_space=pltpu.SMEM)
    vmem = pl.BlockSpec(memory_space=pltpu.VMEM)
    hbm = pl.BlockSpec(memory_space=pl.ANY)
    pan_cells, ms_cells, nodes = pl.pallas_call(
        functools.partial(cell_sums, capacity),
        grid=(n,),
        out_shape=(
            jax.ShapeDtypeStruct((n, pan_rows, pan_cols), BF16),
            jax.ShapeDtypeStruct((n, ms_rows, ms_cols), BF16),
            jax.ShapeDtypeStruct((8, 128), F32),
        ),
        in_specs=[smem, vmem, vmem, vmem, vmem],
        out_specs=(
            pl.BlockSpec((1, pan_rows, pan_cols), lambda t: (t, 0, 0)),
            pl.BlockSpec((1, ms_rows, ms_cols), lambda t: (t, 0, 0)),
            pl.BlockSpec((8, 128), lambda t: (0, 0)),
        ),
        scratch_shapes=[
            pltpu.SMEM((slots,), jnp.int32),
            pltpu.VMEM((pan_rows, pan_cols), F32),
            pltpu.VMEM((ms_rows, ms_cols), F32),
        ],
        name="cell_sums",
    )(send_list, pan_blocks, ms_blocks, row_grid[None, :], col_grid)

    coarse_rows, coarse_cols = TR // 4, TC // 4
    dma = pltpu.SemaphoreType.DMA
    ms_slots = pltpu.VMEM((pairs, 2 * coarse_rows, pan_cols), BF16)
    pan_slots = pltpu.VMEM((pairs, TR, TC), BF16)
    mixed, pan_map = pl.pallas_call(
        functools.partial(mapping, col_grid.shape[1]),
        out_shape=(
            jax.ShapeDtypeStruct((bands, TR, TC), BF16),
            jax.ShapeDtypeStruct((TR, TC), F32),
        ),
        in_specs=[vmem, hbm, hbm, smem, smem, smem],
        out_specs=(hbm, vmem),
        scratch_shapes=[
            pltpu.VMEM((n, pan_rows, pan_cols), BF16),
            pltpu.VMEM((n, ms_rows, ms_cols), BF16),
            pltpu.VMEM((2, n, 8, 128), F32),
            ms_slots,
            ms_slots,
            ms_slots,
            ms_slots,
            pan_slots,
            pan_slots,
            pan_slots,
            pan_slots,
            pltpu.VMEM((2 * coarse_rows, pan_cols), F32),
            pltpu.VMEM((pan_cols, TC), BF16),
            pltpu.VMEM((ms_cols, bands * coarse_cols), BF16),
            pltpu.VMEM((2 * coarse_rows, bands * coarse_cols), BF16),
            pltpu.VMEM((2 * coarse_rows, bands * coarse_cols), BF16),
            pltpu.VMEM((2, coarse_cols, TC), BF16),
            pltpu.VMEM((TR, 2 * coarse_rows), BF16),
            pltpu.VMEM((bands, TR, TC), F32),
            pltpu.VMEM((bands, TR, TC), BF16),
            dma((3,)),
            dma((2, n)),
            dma((2, n)),
        ]
        + [dma((pairs,))] * 8
        + [dma((5,)), dma((5,))],
        compiler_params=pltpu.CompilerParams(
            collective_id=0, has_side_effects=True, vmem_limit_bytes=60 * 1024 * 1024
        ),
        name="mapping",
    )(nodes, pan_cells, ms_cells, band_mix, band_gain, synth_weight)
    detail = band_gain[:, None, None] * pan_map[None]
    return (mixed.astype(F32) + detail).astype(BF16)


def solution(mesh):
    return jax.shard_map(
        local,
        mesh=mesh,
        in_specs=(
            P(("scene", "mrow", "mcol"), None, None),
            P(("scene", "mrow", "mcol"), None, None),
            P(None, ("scene", "mrow", "mcol")),
            P(None, ("scene", "mrow", "mcol")),
            P(("scene", "mrow")),
            P(("scene", "mrow"), "mcol"),
            P(),
            P(),
            P(),
        ),
        out_specs=P(None, ("scene", "mrow"), "mcol"),
        check_vma=False,
    )
```

time: 63.3 us -> 53.3 us (0.84); the launches traced: 62.2 us -> 52.9 us
  Pallas kernels: 57.3 us -> 50.2 us
  local copies, waits for them, and re-layouts: 2.26 us -> 0.01 us
    pallas_call x1, Pallas kernels: 48.4 us -> 41.4 us  [local(): pl.pallas_call(functools.partial(mapping, col_grid.shape[1]), out_shape=(...]
    convert_element_type x0 -> x1, other arithmetic: none -> 2.61 us  [local(): return (mixed.astype(F32) + detail).astype(BF16)]
    unnamed x1 -> x2, local copies, waits for them, and re-layouts: 2.26 us -> 0.01 us
    sub x1 -> x0, other arithmetic: 1.37 us -> none  [local(): jnp.eye(bands, dtype=F32) + band_mix]
    concatenate x1 -> x0, other arithmetic: 1.27 us -> none  [local(): jnp.concatenate([jnp.pad(row_grid[None, :], ((0, 0), (0, 128 - row_grid.s...]
where the time goes in v2:
time: 53.3 us; the launch traced here: 52.9 us
  Pallas kernels  50.2 us (94%)
  other arithmetic  2.61 us (5%)
    pallas_call x1, Pallas kernels, local(): pl.pallas_call(functools.partial(mapping, col_grid.shape[1]), out_shape=(...  41.4 us
    pallas_call x1, Pallas kernels, local(): pl.pallas_call(functools.partial(cell_sums, capacity), grid=(n,), out_sha...  8.8 us
    convert_element_type x1, other arithmetic, local(): return (mixed.astype(F32) + detail).astype(BF16)  2.61 us

profile of v2, /device:TPU:15, one launch (start us, length us, event | category | flops | bytes accessed | tf_op | source)
XLA Modules:
  0.0 52.9 jit_solution(7798884059067533439)
XLA Ops:
  0.0 8.8 %cell_sums.1 = (bf16[8,256,640]{2,1,0:T(8,128)(2,1)}, bf16[8,64,1280]{2,1,0:T(8,128)(2,1)}, f32[8,128]{1,0:T(8,128)}) custom-call(s32[3,64]{1,0:T(4,128)} %send_ref.1, bf16[64,128,128]{2,1,0:T(8,128)(2,1)} %pan_ref.1, bf16[64,32,256]{2,1,0:T(8,128)(2,1)} %ms_ref.1, f32[1,3]{1,0:T(1,128)} %bitcast.1, f32[1,8]{1,0:T(1,128)} %col_ref.1), custom_call_target="tpu_custom_call" | custom-call | tf_op jit(solution)/shard_map/cell_sums/pallas_call | solution.py:493
  8.8 0.0 copy-start
  8.8 41.4 %mapping.1 = (bf16[8,128,512]{2,1,0:T(8,128)(2,1)}, f32[128,512]{1,0:T(8,128)}) custom-call(f32[8,128]{1,0:T(8,128)} %get-tuple-element.10.nodes_ref, bf16[8,256,640]{2,1,0:T(8,128)(2,1)} %get-tuple-element.11.pan_hbm, bf16[8,64,1280]{2,1,0:T(8,128)(2,1)} %get-tuple-element.12.ms_hbm, f32[8,8]{1,0:T(8,128)} %mix_ref.1, f32[8]{0:T(128)} %gain_ref.1, f32[8]{0:T(128)} %synth_ref.1), custom_call_target="tpu_custom_call" | custom-call | tf_op jit(solution)/shard_map/mapping/pallas_call | solution.py:519
  50.2 0.0 copy-done
  50.3 2.6 %add_convert_fusion = bf16[8,128,512]{2,1,0:T(8,128)(2,1)} fusion(bf16[8,128,512]{2,1,0:T(8,128)(2,1)} %get-tuple-element.13, f32[128,512]{1,0:T(8,128)} %get-tuple-element.14, f32[8]{0:T(128)S(1)} %copy-done), kind=kLoop, calls=%fused_computation | loop fusion | flops 2097152 | bytes 2359328 | tf_op jit(solution)/shard_map/convert_element_type | solution.py:560
Async XLA Ops:
  8.8 41.4 %copy-start = (f32[8]{0:T(128)S(1)}, f32[8]{0:T(128)}, u32[]{:S(2)}) copy-start(f32[8]{0:T(128)} %gain_ref.1) | copy-start | bytes 100

commit v3 on v2

--- a/solution.py
+++ b/solution.py
@@ -38,9 +38,8 @@
     pan_out,
     ms_out,
     nodes_out,
-    slot_block,
-    pan_acc,
-    ms_acc,
+    first_block,
+    next_block,
 ):
     tile = pl.program_id(0)
     own_blocks, block_size, _ = pan_ref.shape
@@ -53,44 +52,41 @@
         nodes_out[0:1, 0 : row_ref.shape[1]] = row_ref[...]
         nodes_out[1:2, 0 : col_ref.shape[1]] = col_ref[...]
 
-        def clear(slot, carry):
-            slot_block[slot] = -1
+        def clear(k, carry):
+            for r in range(KR * KC):
+                first_block[k * (KR * KC) + r] = -1
             return carry
 
-        lax.fori_loop(0, slot_block.shape[0], clear, 0)
+        lax.fori_loop(0, first_block.shape[0] // (KR * KC), clear, 0)
 
         def enter(block, carry):
-            slot_block[send_ref[0, block]] = block
+            cell = (send_ref[0, block] // capacity * KR + send_ref[1, block]) * KC
+            cell = cell + send_ref[2, block] - first_col
+            next_block[block] = first_block[cell]
+            first_block[cell] = block
             return carry
 
-        lax.fori_loop(0, own_blocks, enter, 0)
-
-    pan_acc[...] = jnp.zeros_like(pan_acc)
-    ms_acc[...] = jnp.zeros_like(ms_acc)
-
-    def add(slot, carry):
-        block = slot_block[tile * capacity + slot]
-
-        @pl.when(block >= 0)
-        def _():
-            row = send_ref[1, block]
-            col = send_ref[2, block] - first_col
-            at = (
-                pl.ds(pl.multiple_of(row * block_size, block_size), block_size),
-                pl.ds(pl.multiple_of(col * block_size, block_size), block_size),
+        lax.fori_loop(0, own_blocks, enter, 0, unroll=4)
+
+    for row in range(KR):
+        for col in range(KC):
+
+            def add(carry):
+                block, pan, ms = carry
+                pan = pan + pan_ref[block].astype(F32)
+                ms = ms + ms_ref[block].astype(F32)
+                return next_block[block], pan, ms
+
+            start = (
+                first_block[(tile * KR + row) * KC + col],
+                jnp.zeros((block_size, block_size), F32),
+                jnp.zeros((coarse_size, coarse_width), F32),
             )
-            pan_acc[at] += pan_ref[block].astype(F32)
-            at = (
-                pl.ds(pl.multiple_of(row * coarse_size, coarse_size), coarse_size),
-                pl.ds(pl.multiple_of(col * coarse_width, coarse_width), coarse_width),
-            )
-            ms_acc[at] += ms_ref[block].astype(F32)
-
-        return carry
-
-    lax.fori_loop(0, capacity, add, 0)
-    pan_out[0] = pan_acc[...].astype(BF16)
-    ms_out[0] = ms_acc[...].astype(BF16)
+            _, pan, ms = lax.while_loop(lambda carry: carry[0] >= 0, add, start)
+            rows = slice(row * block_size, (row + 1) * block_size)
+            pan_out[0, rows, col * block_size : (col + 1) * block_size] = pan.astype(BF16)
+            rows = slice(row * coarse_size, (row + 1) * coarse_size)
+            ms_out[0, rows, col * coarse_width : (col + 1) * coarse_width] = ms.astype(BF16)
 
 
 def row_coord(nodes, position, offset):
@@ -145,7 +141,6 @@
     beside,
     up_cols,
     up_rows,
-    upsampled,
     mixed,
     load_sem,
     nodes_ss,
@@ -369,7 +364,13 @@
     ms_map = ms_map + jnp.dot(
         right, ms_col_weight[cols : 2 * cols, :], preferred_element_type=F32
     )
-    window[half:mid, :] = ms_map.astype(BF16)
+    values = [ms_map[:, b * coarse_cols : (b + 1) * coarse_cols] for b in range(bands)]
+    synthetic = sum(synth_ref[b] * values[b] for b in range(bands))
+    for b in range(bands):
+        result = values[b] - gain_ref[b] * synthetic
+        for k in range(bands):
+            result = result + mix_ref[b, k] * values[k]
+        window[half:mid, b * coarse_cols : (b + 1) * coarse_cols] = result.astype(BF16)
 
     has_above, has_below = m > 0, m < n - 1
 
@@ -438,21 +439,10 @@
         lanes = slice(b * coarse_cols, (b + 1) * coarse_cols)
         across = jnp.dot(window[:, lanes], up_cols[0], preferred_element_type=F32)
         across = across + jnp.dot(beside[:, lanes], up_cols[1], preferred_element_type=F32)
-        upsampled[b] = jnp.dot(up_rows[...], across.astype(BF16), preferred_element_type=F32)
-
-    def mix_bands(k, carry):
-        rows = pl.ds(pl.multiple_of(k * 16, 16), 16)
-        for lane in range(0, TC, 128):
-            values = [upsampled[b, rows, lane : lane + 128] for b in range(bands)]
-            synthetic = sum(synth_ref[b] * values[b] for b in range(bands))
-            for b in range(bands):
-                result = values[b] - gain_ref[b] * synthetic
-                for k2 in range(bands):
-                    result = result + mix_ref[b, k2] * values[k2]
-                mixed[b, rows, lane : lane + 128] = result.astype(BF16)
-        return carry
-
-    lax.fori_loop(0, TR // 16, mix_bands, 0)
+        mixed[b] = jnp.dot(
+            up_rows[...], across.astype(BF16), preferred_element_type=F32
+        ).astype(BF16)
+
     store = pltpu.make_async_copy(mixed, mixed_hbm, load_sem.at[2])
     store.start()
 
@@ -505,9 +495,8 @@
             pl.BlockSpec((8, 128), lambda t: (0, 0)),
         ),
         scratch_shapes=[
-            pltpu.SMEM((slots,), jnp.int32),
-            pltpu.VMEM((pan_rows, pan_cols), F32),
-            pltpu.VMEM((ms_rows, ms_cols), F32),
+            pltpu.SMEM((n * KR * KC,), jnp.int32),
+            pltpu.SMEM((own_blocks,), jnp.int32),
         ],
         name="cell_sums",
     )(send_list, pan_blocks, ms_blocks, row_grid[None, :], col_grid)
@@ -543,7 +532,6 @@
             pltpu.VMEM((2 * coarse_rows, bands * coarse_cols), BF16),
             pltpu.VMEM((2, coarse_cols, TC), BF16),
             pltpu.VMEM((TR, 2 * coarse_rows), BF16),
-            pltpu.VMEM((bands, TR, TC), F32),
             pltpu.VMEM((bands, TR, TC), BF16),
             dma((3,)),
             dma((2, n)),

time: 53.3 us -> 49.7 us (0.932)
  Pallas kernels: 50.2 us -> 46.8 us
    pallas_call x1, Pallas kernels: 41.4 us -> 39.6 us  [local(): pl.pallas_call(functools.partial(mapping, col_grid.shape[1]), out_shape=(...]
    pallas_call x1, Pallas kernels: 8.8 us -> 7.24 us  [local(): pl.pallas_call(functools.partial(cell_sums, capacity), grid=(n,), out_sha...]
where the time goes in v3:
time: 49.7 us; the launch traced here: 49.4 us
  Pallas kernels  46.8 us (94%)
  other arithmetic  2.61 us (5%)
    pallas_call x1, Pallas kernels, local(): pl.pallas_call(functools.partial(mapping, col_grid.shape[1]), out_shape=(...  39.6 us
    pallas_call x1, Pallas kernels, local(): pl.pallas_call(functools.partial(cell_sums, capacity), grid=(n,), out_sha...  7.24 us
    convert_element_type x1, other arithmetic, local(): return (mixed.astype(F32) + detail).astype(BF16)  2.61 us

profile of v3, /device:TPU:15, one launch (start us, length us, event | category | flops | bytes accessed | tf_op | source)
XLA Modules:
  0.0 49.4 jit_solution(6027097718507027494)
XLA Ops:
  0.0 7.2 %cell_sums.1 = (bf16[8,256,640]{2,1,0:T(8,128)(2,1)}, bf16[8,64,1280]{2,1,0:T(8,128)(2,1)}, f32[8,128]{1,0:T(8,128)}) custom-call(s32[3,64]{1,0:T(4,128)} %send_ref.1, bf16[64,128,128]{2,1,0:T(8,128)(2,1)} %pan_ref.1, bf16[64,32,256]{2,1,0:T(8,128)(2,1)} %ms_ref.1, f32[1,3]{1,0:T(1,128)} %bitcast.1, f32[1,8]{1,0:T(1,128)} %col_ref.1), custom_call_target="tpu_custom_call" | custom-call | tf_op jit(solution)/shard_map/cell_sums/pallas_call | solution.py:483
  7.2 0.0 copy-start
  7.2 39.6 %mapping.1 = (bf16[8,128,512]{2,1,0:T(8,128)(2,1)}, f32[128,512]{1,0:T(8,128)}) custom-call(f32[8,128]{1,0:T(8,128)} %get-tuple-element.10.nodes_ref, bf16[8,256,640]{2,1,0:T(8,128)(2,1)} %get-tuple-element.11.pan_hbm, bf16[8,64,1280]{2,1,0:T(8,128)(2,1)} %get-tuple-element.12.ms_hbm, f32[8,8]{1,0:T(8,128)} %mix_ref.1, f32[8]{0:T(128)} %gain_ref.1, f32[8]{0:T(128)} %synth_ref.1), custom_call_target="tpu_custom_call" | custom-call | tf_op jit(solution)/shard_map/mapping/pallas_call | solution.py:508
  46.8 0.0 copy-done
  46.8 2.6 %add_convert_fusion = bf16[8,128,512]{2,1,0:T(8,128)(2,1)} fusion(bf16[8,128,512]{2,1,0:T(8,128)(2,1)} %get-tuple-element.13, f32[128,512]{1,0:T(8,128)} %get-tuple-element.14, f32[8]{0:T(128)S(1)} %copy-done), kind=kLoop, calls=%fused_computation | loop fusion | flops 2097152 | bytes 2359328 | tf_op jit(solution)/shard_map/convert_element_type | solution.py:548
Async XLA Ops:
  7.2 39.6 %copy-start = (f32[8]{0:T(128)S(1)}, f32[8]{0:T(128)}, u32[]{:S(2)}) copy-start(f32[8]{0:T(128)} %gain_ref.1) | copy-start | bytes 100

commit v4 on v3

--- a/solution.py
+++ b/solution.py
@@ -31,8 +31,8 @@
 def cell_sums(
     capacity,
     send_ref,
-    pan_ref,
-    ms_ref,
+    pan_hbm,
+    ms_hbm,
     row_ref,
     col_ref,
     pan_out,
@@ -40,6 +40,9 @@
     nodes_out,
     first_block,
     next_block,
+    pan_ref,
+    ms_ref,
+    load_sem,
 ):
     tile = pl.program_id(0)
     own_blocks, block_size, _ = pan_ref.shape
@@ -48,6 +51,10 @@
 
     @pl.when(tile == 0)
     def _():
+        pan_load = pltpu.make_async_copy(pan_hbm, pan_ref, load_sem.at[0])
+        ms_load = pltpu.make_async_copy(ms_hbm, ms_ref, load_sem.at[1])
+        pan_load.start()
+        ms_load.start()
         nodes_out[...] = jnp.zeros_like(nodes_out)
         nodes_out[0:1, 0 : row_ref.shape[1]] = row_ref[...]
         nodes_out[1:2, 0 : col_ref.shape[1]] = col_ref[...]
@@ -67,6 +74,8 @@
             return carry
 
         lax.fori_loop(0, own_blocks, enter, 0, unroll=4)
+        pan_load.wait()
+        ms_load.wait()
 
     for row in range(KR):
         for col in range(KC):
@@ -488,7 +497,7 @@
             jax.ShapeDtypeStruct((n, ms_rows, ms_cols), BF16),
             jax.ShapeDtypeStruct((8, 128), F32),
         ),
-        in_specs=[smem, vmem, vmem, vmem, vmem],
+        in_specs=[smem, hbm, hbm, vmem, vmem],
         out_specs=(
             pl.BlockSpec((1, pan_rows, pan_cols), lambda t: (t, 0, 0)),
             pl.BlockSpec((1, ms_rows, ms_cols), lambda t: (t, 0, 0)),
@@ -497,6 +506,9 @@
         scratch_shapes=[
             pltpu.SMEM((n * KR * KC,), jnp.int32),
             pltpu.SMEM((own_blocks,), jnp.int32),
+            pltpu.VMEM(pan_blocks.shape, BF16),
+            pltpu.VMEM(ms_blocks.shape, BF16),
+            pltpu.SemaphoreType.DMA((2,)),
         ],
         name="cell_sums",
     )(send_list, pan_blocks, ms_blocks, row_grid[None, :], col_grid)

time: 49.7 us -> 49.5 us (level)
  no operation moved by 1% of the time
where the time goes in v4:
time: 49.5 us; the launch traced here: 49.1 us
  Pallas kernels  46.4 us (94%)
  other arithmetic  2.61 us (5%)
    pallas_call x1, Pallas kernels, local(): pl.pallas_call(functools.partial(mapping, col_grid.shape[1]), out_shape=(...  39.6 us
    pallas_call x1, Pallas kernels, local(): pl.pallas_call(functools.partial(cell_sums, capacity), grid=(n,), out_sha...  6.81 us
    convert_element_type x1, other arithmetic, local(): return (mixed.astype(F32) + detail).astype(BF16)  2.61 us

profile of v4, /device:TPU:15, one launch (start us, length us, event | category | flops | bytes accessed | tf_op | source)
XLA Modules:
  0.0 49.1 jit_solution(4221910485549029254)
XLA Ops:
  0.0 6.8 %cell_sums.1 = (bf16[8,256,640]{2,1,0:T(8,128)(2,1)}, bf16[8,64,1280]{2,1,0:T(8,128)(2,1)}, f32[8,128]{1,0:T(8,128)}) custom-call(s32[3,64]{1,0:T(4,128)} %send_ref.1, bf16[64,128,128]{2,1,0:T(8,128)(2,1)} %pan_hbm.1, bf16[64,32,256]{2,1,0:T(8,128)(2,1)} %ms_hbm.1, f32[1,3]{1,0:T(1,128)} %bitcast.1, f32[1,8]{1,0:T(1,128)} %col_ref.1), custom_call_target="tpu_custom_call" | custom-call | tf_op jit(solution)/shard_map/cell_sums/pallas_call | solution.py:492
  6.8 0.0 copy-start
  6.8 39.6 %mapping.1 = (bf16[8,128,512]{2,1,0:T(8,128)(2,1)}, f32[128,512]{1,0:T(8,128)}) custom-call(f32[8,128]{1,0:T(8,128)} %get-tuple-element.10.nodes_ref, bf16[8,256,640]{2,1,0:T(8,128)(2,1)} %get-tuple-element.11.pan_hbm, bf16[8,64,1280]{2,1,0:T(8,128)(2,1)} %get-tuple-element.12.ms_hbm, f32[8,8]{1,0:T(8,128)} %mix_ref.1, f32[8]{0:T(128)} %gain_ref.1, f32[8]{0:T(128)} %synth_ref.1), custom_call_target="tpu_custom_call" | custom-call | tf_op jit(solution)/shard_map/mapping/pallas_call | solution.py:520
  46.5 0.0 copy-done
  46.5 2.6 %add_convert_fusion = bf16[8,128,512]{2,1,0:T(8,128)(2,1)} fusion(bf16[8,128,512]{2,1,0:T(8,128)(2,1)} %get-tuple-element.13, f32[128,512]{1,0:T(8,128)} %get-tuple-element.14, f32[8]{0:T(128)S(1)} %copy-done), kind=kLoop, calls=%fused_computation | loop fusion | flops 2097152 | bytes 2359328 | tf_op jit(solution)/shard_map/convert_element_type | solution.py:560
Async XLA Ops:
  6.8 39.7 %copy-start = (f32[8]{0:T(128)S(1)}, f32[8]{0:T(128)}, u32[]{:S(2)}) copy-start(f32[8]{0:T(128)} %gain_ref.1) | copy-start | bytes 100
